TPU v7x, 32 devices: a whole 2x2x4 slice. The times are simulated.
32 devices in a mesh: kz: 4 (over x, core), tile: 8 (over z, y).
Axes of the slice: x: 2, y: 2, z: 4, core: 2. Of those that a mesh axis runs over, the one named last changes fastest.
Arguments:
- coil_data: bfloat16 [4, 8, 4, 8, 2, 16, 128], P('kz', 'tile'), may hold values from -6 to 6
- frame_of: int32 [4, 8, 4, 8, 2], P('kz', 'tile'), may hold values from 0 to 999
- basis: bfloat16 [1000, 10], replicated, may hold values from -4 to 4
- sample_pos: float32 [4, 8, 4, 8, 2, 2, 128], P('kz', 'tile'), may hold values from 1.5 to 30.5, as said below
- window_at: int32 [4, 8, 4, 8, 2, 2], P('kz', 'tile'), may hold values from -2 to 639, as said below
- live_count: int32 [4, 8, 4, 8], P('kz', 'tile'), may hold values from 0 to 2, as said below
Outputs:
- image: bfloat16 [4, 640, 102400], P('kz', None, 'tile')
Inputs may be any that keep to these rules, and one draw needn't show every extreme that they name: `live_count`: live slots of a pair are its first ones; destination tiles from 3 up to but not including 8 * 5 // 8 receive every slot from every acquiring device. `window_at`: the first entry (row0) lies in -2 to 78, the second (col0) in 0 to 639. `sample_pos`: the first entry lies in 1.5 to 2.5, the second in 1.5 to 32 - 1.5.
All inputs are finite; a program needn't handle non-finite values.
Results may differ from a plain program's by a relative error of at most 0.0077.
Values may be sent and summed in bfloat16 or wider, within the bound.
No kernel may reach another device: no remote copies, remote signals or barrier semaphores. Data moves between devices by JAX's collectives and lax.ppermute only.
A program may use at most 192 MiB of HBM per device.

v0:
```python
import functools
import math

import jax
import jax.numpy as jnp
import numpy as np
from jax import lax
from jax.experimental import pallas as pl
from jax.experimental.pallas import tpu as pltpu
from jax.sharding import PartitionSpec as P


PLANE = 640
WIN_ROWS = 4
WIN_COLS = 32
LANES = 128
NOTES = 16
ROW_NOTE = 13
COL_HIGH = 14
COL_LOW = 15
COL_STEP = 32
FAR_OFF = -1000.0
CHUNK = 256
NT_DIMS = (((1,), (1,)), ((), ()))


def taper(dist):
    inner = 1.0 - (dist / 1.5) ** 2
    return jnp.maximum(inner, 0.0) ** 2


def wave_tables():
    idx = np.arange(PLANE)
    phase = (idx[:, None] * idx[None, :] % PLANE) * (2.0 * math.pi / PLANE)
    return np.cos(phase).astype(jnp.bfloat16), np.sin(phase).astype(jnp.bfloat16)


def dot_nt(left, right):
    return lax.dot_general(left, right, NT_DIMS, preferred_element_type=jnp.float32)


def unit(shape, dtype=jnp.bfloat16):
    return (lax.broadcasted_iota(jnp.int32, shape, 0) == lax.broadcasted_iota(jnp.int32, shape, 1)).astype(jnp.float32).astype(dtype)


def table_kernel(coils, wave_ref, rows_ref, lanes_ref, out_ref, waves_ref):
    ys = rows_ref.shape[0]
    plane = wave_ref.shape[0]
    rows, width = out_ref.shape
    spot = lax.broadcasted_iota(jnp.int32, (LANES, width), 0)
    lane = lax.broadcasted_iota(jnp.int32, (LANES, width), 1)
    pick = (spot == lane % WIN_COLS).astype(jnp.float32).astype(jnp.bfloat16)
    cos_y = jnp.dot(rows_ref[:, :LANES], pick, preferred_element_type=jnp.float32)
    sin_y = jnp.dot(rows_ref[:, plane : plane + LANES], pick, preferred_element_type=jnp.float32)
    lane = lax.broadcasted_iota(jnp.int32, (ys, width), 1) // WIN_COLS
    into_re = jnp.where(lane < coils, cos_y, -sin_y)
    into_im = jnp.where(lane < coils, sin_y, cos_y)
    both = jnp.concatenate([into_re[:, None, None, :], into_im[:, None, None, :]], axis=1)
    both = jnp.broadcast_to(both, (ys, 2, coils, width))
    mine = lax.broadcasted_iota(jnp.int32, both.shape, 2)
    other = lax.broadcasted_iota(jnp.int32, both.shape, 3) // WIN_COLS % coils
    out_ref[...] = jnp.where(mine == other, both, 0.0).reshape(rows, width).astype(jnp.bfloat16)

    half, double = waves_ref.shape[1:]
    held = double // 2
    row = lax.broadcasted_iota(jnp.int32, (plane, held), 0)
    for parity in range(2):
        pick = (row == lanes_ref[parity : parity + 1, :]).astype(jnp.float32).astype(jnp.bfloat16)
        for part in range(2):
            waves_ref[parity, :, part * held : (part + 1) * held] = jnp.dot(
                wave_ref[:half, part * plane : (part + 1) * plane], pick, preferred_element_type=jnp.float32
            ).astype(jnp.bfloat16)


def make_tables(wave, wave_rows, lane_rows, coils):
    ys = wave_rows.shape[0]
    plane = wave.shape[0]
    return pl.pallas_call(
        functools.partial(table_kernel, coils),
        out_shape=[
            jax.ShapeDtypeStruct((ys * 2 * coils, WIN_COLS * 2 * coils), jnp.bfloat16),
            jax.ShapeDtypeStruct((2, plane // 2, 2 * lane_rows.shape[1]), jnp.bfloat16),
        ],
        compiler_params=pltpu.CompilerParams(vmem_limit_bytes=40 << 20),
        name="make_tables",
    )(wave, wave_rows, lane_rows)


def pack_kernel(frame_ref, data_ref, basis_ref, out_ref, rows_ref, rates_ref):
    parts, tiles, slots, pair, samples = data_ref.shape[2:]
    devices = parts * tiles
    rows_ref[...] = lax.dot_general(
        basis_ref[...], unit((basis_ref.shape[0], samples)), (((0,), (0,)), ((), ())), preferred_element_type=jnp.float32
    )
    out_ref[:, : slots * pair, :] = data_ref[...].reshape(devices, slots * pair, samples)
    rates_ref[...] = jnp.zeros_like(rates_ref)

    @pl.loop(0, parts)
    def _(part):
        for tile in range(tiles):
            for slot in range(slots):
                frame = frame_ref[0, 0, part, slot, tile]
                row = (part * tiles + tile) * (slots * WIN_ROWS) + slot * WIN_ROWS
                rates_ref[pl.ds(row, 1), :] = rows_ref[pl.ds(frame, 1), :]

    out_ref[:, slots * pair :, :] = rates_ref[...].reshape(devices, slots * WIN_ROWS, samples).astype(jnp.bfloat16)


def pack_slots(coil_data, frame_of, basis):
    parts, tiles, slots, pair, samples = coil_data.shape[2:]
    devices = parts * tiles
    return pl.pallas_call(
        pack_kernel,
        in_specs=[
            pl.BlockSpec(memory_space=pltpu.SMEM),
            pl.BlockSpec(memory_space=pltpu.VMEM),
            pl.BlockSpec(memory_space=pltpu.VMEM),
        ],
        out_shape=jax.ShapeDtypeStruct((devices, slots * (pair + WIN_ROWS), samples), jnp.bfloat16),
        scratch_shapes=[
            pltpu.VMEM((basis.shape[0], samples), jnp.float32),
            pltpu.VMEM((devices * slots * WIN_ROWS, samples), jnp.float32),
        ],
        compiler_params=pltpu.CompilerParams(vmem_limit_bytes=60 << 20),
        name="pack_slots",
    )(jnp.swapaxes(frame_of, 3, 4), coil_data, basis.T)


def window_kernel(slots, pair, data_ref, rate_ref, weight_ref, place_ref, out_ref, held, rates):
    sources = data_ref.shape[0]
    count = held.shape[0] // pair
    step = pl.program_id(0)
    for q in range(sources * slots):
        data = data_ref[q // slots, (q % slots) * pair : (q % slots + 1) * pair]
        first = (step * sources * slots + q) * pair
        held[pl.ds(pl.multiple_of(first, pair), pair), :] = dot_nt(data, weight_ref[q])

    @pl.when(step == pl.num_programs(0) - 1)
    def _():
        depth = place_ref.shape[1]
        width = out_ref.shape[1]
        per = LANES // WIN_COLS
        lane = lax.broadcasted_iota(jnp.int32, (count, LANES), 1) // WIN_COLS
        for group in range(pair // per):
            rows = [held[pl.ds(group * per + q, count, stride=pair), :] for q in range(per)]
            for i in range(WIN_ROWS):
                total = None
                for q in range(per):
                    turn = (q - i) % per * WIN_COLS
                    moved = pltpu.roll(rows[q], turn, 1) if turn else rows[q]
                    total = moved if total is None else jnp.where(lane == q, moved, total)
                out_ref[i * count : (i + 1) * count, group * LANES : (group + 1) * LANES] = total.astype(jnp.bfloat16)
        rates[...] = rate_ref[...].astype(jnp.float32).reshape(rates.shape)
        once = rates[pl.ds(0, count, stride=WIN_ROWS), :].astype(jnp.bfloat16)
        notes = dot_nt(unit((NOTES, LANES)), jnp.concatenate([once] * WIN_ROWS, axis=0)) + place_ref[...]
        lanes = min(depth, width)
        for part in range(depth // lanes):
            part_rows = notes[:, part * lanes : (part + 1) * lanes]
            if lanes < width:
                part_rows = jnp.concatenate([part_rows, jnp.zeros((NOTES, width - lanes), jnp.float32)], axis=1)
            out_ref[depth + part * NOTES : depth + (part + 1) * NOTES, :] = part_rows.astype(jnp.bfloat16)


def grid_windows(raw, weights, place, slots, pair):
    devices, _, samples = raw.shape
    count = devices * slots
    depth = count * WIN_ROWS
    width = WIN_COLS * pair
    sources = 8
    rate_rows = slots * WIN_ROWS
    total_rows = depth + NOTES * (depth // min(depth, width))
    return pl.pallas_call(
        functools.partial(window_kernel, slots, pair),
        grid=(devices // sources,),
        in_specs=[
            pl.BlockSpec((sources, slots * pair, samples), lambda s: (s, 0, 0)),
            pl.BlockSpec((devices, rate_rows, samples), lambda s: (0, slots * pair // rate_rows, 0)),
            pl.BlockSpec((sources * slots, LANES, samples), lambda s: (s, 0, 0)),
            pl.BlockSpec((NOTES, depth), lambda s: (0, 0)),
        ],
        out_specs=pl.BlockSpec((total_rows, width), lambda s: (0, 0)),
        out_shape=jax.ShapeDtypeStruct((total_rows, width), jnp.bfloat16),
        scratch_shapes=[
            pltpu.VMEM((count * pair, LANES), jnp.float32),
            pltpu.VMEM((devices * rate_rows, LANES), jnp.float32),
        ],
        compiler_params=pltpu.CompilerParams(vmem_limit_bytes=24 << 20),
        name="grid_windows",
    )(raw, raw, weights, place)


def columns_kernel(coils, odd_ref, mine_ref, mine_notes, other_ref, other_notes, table_ref, wave_ref, out_ref, notes_ref):
    rows = table_ref.shape[0]
    ys = rows // (2 * coils)
    plane = wave_ref.shape[1] // 2
    depth = mine_ref.shape[0]
    take_mine = odd_ref[0] == pl.program_id(0)
    grids = jnp.where(take_mine, mine_ref[...], other_ref[...])
    notes = jnp.where(take_mine, mine_notes[...], other_notes[...])
    notes_ref[0] = notes
    notes = notes.astype(jnp.float32)
    col0 = notes[COL_HIGH : COL_HIGH + 1] * COL_STEP + notes[COL_LOW : COL_LOW + 1]
    row = lax.broadcasted_iota(jnp.int32, (plane, depth), 0).astype(jnp.float32)
    corner = (row == col0).astype(jnp.float32).astype(jnp.bfloat16)
    turn_re = jnp.dot(wave_ref[:, :plane], corner, preferred_element_type=jnp.float32)[:, None, :]
    turn_im = jnp.dot(wave_ref[:, plane:], corner, preferred_element_type=jnp.float32)[:, None, :]
    flat = dot_nt(table_ref[...], grids).reshape(ys, 2, coils, depth)
    real, imag = flat[:, 0], flat[:, 1]
    done_re = real * turn_re - imag * turn_im
    done_im = real * turn_im + imag * turn_re
    both = jnp.concatenate([done_re[:, None], done_im[:, None]], axis=1)
    out_ref[0] = both.reshape(rows, depth).astype(jnp.bfloat16)


def transform_columns(odd, mine, other, table, wave_rows, depth, coils):
    width = mine.shape[1]
    rows = table.shape[0]
    ys, waves = wave_rows.shape
    chunk = min(depth, CHUNK)
    per = depth // chunk
    grid_spec = pl.BlockSpec((chunk, width), lambda e, k: (k, 0))
    note_spec = pl.BlockSpec(
        (NOTES, chunk), lambda e, k: (depth // NOTES + k * chunk // width, k * chunk % width // chunk)
    )
    return pl.pallas_call(
        functools.partial(columns_kernel, coils),
        grid=(2, per),
        in_specs=[
            pl.BlockSpec(memory_space=pltpu.SMEM),
            grid_spec,
            note_spec,
            grid_spec,
            note_spec,
            pl.BlockSpec((rows, width), lambda e, k: (0, 0)),
            pl.BlockSpec((ys, waves), lambda e, k: (0, 0)),
        ],
        out_specs=[
            pl.BlockSpec((1, rows, chunk), lambda e, k: (e, 0, k)),
            pl.BlockSpec((1, NOTES, chunk), lambda e, k: (e, 0, k)),
        ],
        out_shape=[
            jax.ShapeDtypeStruct((2, rows, depth), jnp.bfloat16),
            jax.ShapeDtypeStruct((2, NOTES, depth), jnp.bfloat16),
        ],
        compiler_params=pltpu.CompilerParams(vmem_limit_bytes=28 << 20),
        cost_estimate=pl.CostEstimate(
            flops=2 * 2 * rows * width * depth, bytes_accessed=2 * 2 * rows * depth, transcendentals=0
        ),
        name="transform_columns",
    )(odd, mine, mine, other, other, table, wave_rows)


def rows_kernel(seats, second, ranks, coils, *refs):
    near = len(seats)
    mids = refs[:near]
    notes = refs[near : 2 * near]
    out_ref = refs[2 * near]
    held = refs[2 * near + 1] if len(refs) > 2 * near + 1 else None
    _, rows, chunk = mids[0].shape
    groups = rows // coils
    step = pl.program_id(0)
    left = jnp.concatenate([mid[0] for mid in mids], axis=1)
    half = LANES // 2
    lane = lax.broadcasted_iota(jnp.int32, (LANES, chunk), 0)
    odd = (lane >= half) if not second else (lane < half)
    spot = (2 * (lane % half + half * second) + odd.astype(jnp.int32)).astype(jnp.float32)
    told = [note[0].astype(jnp.float32) for note in notes]
    hits = [told[d][ROW_NOTE : ROW_NOTE + 1] + 2.0 * seats[d] == spot for d in range(near)]

    def finish(pair, total):
        low = total[:, :LANES].reshape(groups, 1, coils, LANES)
        high = total[:, LANES:].reshape(groups, 1, coils, LANES)
        both = jnp.concatenate([low, high], axis=1).reshape(groups, 2 * coils, LANES)
        out_ref[:, pair] = both.astype(jnp.bfloat16)

    for pair in range(ranks // 2):
        right = jnp.concatenate(
            [
                jnp.concatenate(
                    [jnp.where(hits[d], told[d][rank : rank + 1], 0.0).astype(jnp.bfloat16) for d in range(near)], axis=1
                )
                for rank in (2 * pair, 2 * pair + 1)
            ],
            axis=0,
        )
        total = dot_nt(left, right)
        if held is None:
            finish(pair, total)
        else:

            @pl.when(step == 0)
            def _(pair=pair, total=total):
                held[pair] = total

            @pl.when(step > 0)
            def _(pair=pair, total=total):
                held[pair] += total

            @pl.when(step == pl.num_programs(0) - 1)
            def _(pair=pair):
                finish(pair, held[pair])


def expand_rows(mids, notes, picks, seats, second, ranks, coils):
    _, rows, depth = mids[0].shape
    near = len(mids)
    chunk = min(depth, CHUNK)
    per = depth // chunk
    groups = rows // coils
    shape = (groups, ranks // 2, 2 * coils, LANES)
    return pl.pallas_call(
        functools.partial(rows_kernel, seats, second, ranks, coils),
        grid=(per,),
        in_specs=[
            *(pl.BlockSpec((1, rows, chunk), lambda k, e=e: (e, 0, k)) for e in picks),
            *(pl.BlockSpec((1, NOTES, chunk), lambda k, e=e: (e, 0, k)) for e in picks),
        ],
        out_specs=pl.BlockSpec(shape, lambda k: (0, 0, 0, 0)),
        out_shape=jax.ShapeDtypeStruct(shape, jnp.bfloat16),
        scratch_shapes=[pltpu.VMEM((ranks // 2, rows, 2 * LANES), jnp.float32)] if per > 1 else [],
        compiler_params=pltpu.CompilerParams(vmem_limit_bytes=28 << 20),
        cost_estimate=pl.CostEstimate(
            flops=2 * rows * near * depth * ranks * LANES, bytes_accessed=2 * rows * ranks * LANES, transcendentals=0
        ),
        name="expand_rows",
    )(*mids, *notes)


def image_kernel(*refs):
    waves_ref, out_ref = refs[-2:]
    plane = out_ref.shape[0]
    half = plane // 2
    firsts = [ref[...] for ref in refs[:-2:2]]
    seconds = [ref[...] for ref in refs[1:-2:2]]
    groups, pairs, inner, _ = firsts[0].shape
    columns = groups * pairs * inner
    lower = lax.broadcasted_iota(jnp.int32, firsts[0].shape, 3) < LANES // 2
    sums = []
    for parity in range(2):
        chosen = zip(firsts, seconds) if parity == 0 else zip(seconds, firsts)
        block = jnp.concatenate([jnp.where(lower, a, b) for a, b in chosen], axis=-1)
        lanes = block.shape[-1]
        block = block.reshape(groups // 2, 2, pairs * inner, lanes)
        crossed = jnp.concatenate([-block[:, 1:2], block[:, 0:1]], axis=1)
        right = jnp.concatenate([block.reshape(columns, lanes), crossed.reshape(columns, lanes)], axis=1)
        sums.append(dot_nt(waves_ref[parity], right))
    out_ref[:half, :] = ((sums[0] + sums[1]) * (1.0 / plane)).astype(jnp.bfloat16)
    out_ref[half:, :] = ((sums[0] - sums[1]) * (1.0 / plane)).astype(jnp.bfloat16)


def form_image(blocks, waves):
    plane = 2 * waves.shape[1]
    groups, pairs, inner, _ = blocks[0].shape
    step = next(n for n in (16, 8, 4, 2) if groups % n == 0)
    columns = step * pairs * inner
    return pl.pallas_call(
        image_kernel,
        grid=(groups // step,),
        in_specs=[
            *(pl.BlockSpec((step, pairs, inner, LANES), lambda s: (s, 0, 0, 0)) for _ in blocks),
            pl.BlockSpec(waves.shape, lambda s: (0, 0, 0)),
        ],
        out_specs=pl.BlockSpec((plane, columns), lambda s: (0, s)),
        out_shape=jax.ShapeDtypeStruct((plane, groups * pairs * inner), jnp.bfloat16),
        compiler_params=pltpu.CompilerParams(vmem_limit_bytes=24 << 20),
        cost_estimate=pl.CostEstimate(
            flops=2 * plane * waves.shape[2] * groups * pairs * inner,
            bytes_accessed=4 * plane * groups * pairs * inner,
            transcendentals=0,
        ),
        name="form_image",
    )(*blocks, waves)


def pack_tiles(tiles, tile_rows):
    span = (tile_rows + WIN_ROWS) // 2
    room = LANES // span
    twos = []
    for first in range(0, tiles, room):
        members = list(range(first, min(first + room, tiles)))
        stride = LANES // 2 if len(members) <= 2 and span <= LANES // 2 else span
        twos.append([(t, n * stride) for n, t in enumerate(members)])
    return twos, span


def kx_of_lanes(twos, span):
    at = np.full((2, 2, len(twos) * LANES), -1, np.int32)
    for n, members in enumerate(twos):
        for t, seat in members:
            for k in range(span):
                even = seat + k
                odd = (seat + k + LANES // 2) % LANES
                at[:, 0, n * LANES + even] = t, 2 * k
                at[:, 1, n * LANES + odd] = t, 2 * k + 1
    return at


def from_tiles(value, source_of):
    count = lax.axis_size("tile")
    return lax.ppermute(value, "tile", [(source_of(t), t) for t in range(count)])


def body(coil_data, frame_of, basis, sample_pos, window_at, live_count):
    parts = coil_data.shape[2]
    tiles = coil_data.shape[3]
    slots = coil_data.shape[4]
    pair = coil_data.shape[5]
    samples = coil_data.shape[6]
    coils = pair // 2
    ranks = basis.shape[1]
    tile_rows = PLANE // tiles
    devices = parts * tiles
    count = devices * slots
    depth = count * WIN_ROWS
    ys = PLANE // tiles
    my_tile = lax.axis_index("tile")
    odd = my_tile % 2

    packed = pack_slots(coil_data, frame_of, basis)
    raw = lax.all_to_all(packed, ("kz", "tile"), split_axis=0, concat_axis=0, tiled=True)

    counts = live_count.reshape(devices)
    slot_idx = jnp.arange(slots, dtype=jnp.int32)
    alive = (slot_idx[None, :] < counts[:, None]).reshape(count, 1, 1)
    pos = jnp.where(alive, sample_pos.reshape(count, 2, samples), FAR_OFF)
    row_k = taper(jnp.arange(WIN_ROWS, dtype=jnp.float32)[None, :, None] - pos[:, 0:1, :])
    col_k = taper(jnp.arange(WIN_COLS, dtype=jnp.float32)[None, :, None] - pos[:, 1:2, :])
    weights = row_k[:, :, None, :] * col_k[:, None, :, :]
    weights = weights.reshape(count, WIN_ROWS * WIN_COLS, samples).astype(jnp.bfloat16)
    corners = window_at.reshape(count, 2)
    win_row = jnp.arange(WIN_ROWS, dtype=jnp.int32)
    from_row = (2 + corners[None, :, 0] + win_row[:, None]).reshape(1, depth)
    col0 = jnp.tile(corners[:, 1], WIN_ROWS).reshape(1, depth)
    place = jnp.concatenate([from_row, col0 // COL_STEP, col0 % COL_STEP], axis=0).astype(jnp.float32)
    place = jnp.pad(place, ((ROW_NOTE, NOTES - ROW_NOTE - 3), (0, 0)))

    cos_tab, sin_tab = wave_tables()
    wave = jnp.asarray(np.concatenate([cos_tab, sin_tab], axis=1))
    wave_rows = lax.dynamic_slice_in_dim(wave, my_tile * ys, ys, 0)
    twos, span = pack_tiles(tiles, tile_rows)
    arrival, window_row = (jnp.asarray(part) for part in kx_of_lanes(twos, span))
    lane_tile = (arrival // 2 ^ my_tile // 2) * 2 + arrival % 2
    lane_rows = jnp.where(arrival < 0, -1, (lane_tile * tile_rows - 2 + window_row + PLANE) % PLANE)
    table, waves = make_tables(wave, wave_rows, lane_rows, coils)

    raw, weights, place, table, waves = lax.optimization_barrier((raw, weights, place, table, waves))
    windows = grid_windows(raw, weights, place, slots, pair)

    pairs = tiles // 2
    mine, other = [windows], []
    for hop in range(1, pairs):
        near = hop & -hop
        mine.append(from_tiles(mine[hop - near], lambda t, near=near: (t // 2 ^ near) * 2 + t % 2))
    for hop in range(pairs):
        other.append(from_tiles(mine[hop], lambda t: t // 2 * 2 + 1 - t % 2))
    odd_ref = odd.astype(jnp.int32).reshape(1)
    mids, notes = [], []
    for hop in range(pairs):
        mid, note = transform_columns(odd_ref, mine[hop], other[hop], table, wave_rows, depth, coils)
        mids.append(mid)
        notes.append(note)

    blocks = []
    for members in twos:
        for second in range(2):
            low, high = second * (LANES // 2), (second + 1) * (LANES // 2)
            met = [(t, seat) for t, seat in members if seat < high and seat + span > low]
            block = expand_rows(
                [mids[t // 2] for t, _ in met],
                [notes[t // 2] for t, _ in met],
                [t % 2 for t, _ in met],
                [float(seat) for _, seat in met],
                second,
                ranks,
                coils,
            )
            blocks.append(block)
    return form_image(blocks, waves)[None]


def solution(mesh):
    return jax.shard_map(
        body,
        mesh=mesh,
        in_specs=(
            P("kz", "tile", None, None, None, None, None),
            P("kz", "tile", None, None, None),
            P(),
            P("kz", "tile", None, None, None, None, None),
            P("kz", "tile", None, None, None, None),
            P("kz", "tile", None, None),
        ),
        out_specs=P("kz", None, "tile"),
        check_vma=False,
    )
```

profile of v0, /device:TPU:0, one launch (start us, length us, event | category | flops | bytes accessed | tf_op | source)
XLA Modules:
  0.0 82.2 jit_solution(4144918667983447750)
XLA Ops:
  0.0 2.2 %pack_slots.1 = bf16[32,40,128]{2,1,0:T(8,128)(2,1)} custom-call(s32[1,1,4,2,8]{4,3,2,1,0:T(2,128)} %bitcast.21, bf16[1,1,4,8,2,16,128]{6,5,4,3,2,1,0:T(8,128)(2,1)} %data_ref.1, bf16[10,1000]{1,0:T(8,128)(2,1)} %bitcast.20), custom_call_target="tpu_custom_call" | custom-call | tf_op jit(solution)/shard_map/pack_slots/pallas_call | solution.py:112
  2.2 7.4 %all-to-all-start = ((bf16[32,40,128]{2,1,0:T(8,128)(2,1)}), bf16[32,40,128]{2,1,0:T(8,128)(2,1)}, u32[]{:S(2)}, u32[]{:S(2)}) async-start(bf16[32,40,128]{2,1,0:T(8,128)(2,1)} %pack_slots.1), calls=%async_computation | async-start | bytes 655360 | tf_op jit(solution)/shard_map/all_to_all | solution.py:420
  11.8 1.0 %bitcast_select_fusion = f32[64,2,128]{2,1,0:T(2,128)S(1)} fusion(f32[1,1,4,8,2,2,128]{6,5,4,3,2,1,0:T(2,128)} %param.12, pred[64]{0:T(512)(128)(4,1)S(1)} %lt.60), kind=kLoop, calls=%fused_computation.3 | loop fusion | flops 16384 | bytes 131136 | tf_op jit(solution)/shard_map/jit(_where)/select_n | solution.py:425
  12.9 1.0 %constant_dynamic-slice_fusion.rows_ref.wave_ref = bf16[80,1280]{1,0:T(8,128)(2,1)S(1)} fusion(bf16[640,1280]{1,0:T(8,128)(2,1)} %constant.112.clone.wave_ref, s32[]{:T(128)S(6)} %select_n.70), kind=kLoop, calls=%fused_computation.16 | loop fusion | bytes 409604 | tf_op jit(solution)/shard_map/dynamic_slice | solution.py:439
  14.7 1.5 %make_tables.1 = (bf16[1280,512]{1,0:T(8,128)(2,1)S(1)}, bf16[2,320,768]{2,1,0:T(8,128)(2,1)S(1)}) custom-call(bf16[640,1280]{1,0:T(8,128)(2,1)S(1)} %copy-done.3, bf16[80,1280]{1,0:T(8,128)(2,1)S(1)} %constant_dynamic-slice_fusion.rows_ref.wave_ref, s32[2,384]{1,0:T(2,128)S(1)} %fusion.lanes_ref), custom_call_target="tpu_custom_call" | custom-call | tf_op jit(solution)/shard_map/make_tables/pallas_call | solution.py:78
  17.8 3.9 %all-to-all-done.data_ref.rate_ref = bf16[32,40,128]{2,1,0:T(8,128)(2,1)} async-done(((bf16[32,40,128]{2,1,0:T(8,128)(2,1)}), bf16[32,40,128]{2,1,0:T(8,128)(2,1)}, u32[]{:S(2)}, u32[]{:S(2)}) %all-to-all-start) | async-done | bytes 327712 | tf_op jit(solution)/shard_map/all_to_all | solution.py:420
  21.7 3.9 %grid_windows.1.mine_ref.mine_notes = bf16[272,512]{1,0:T(8,128)(2,1)} custom-call(bf16[32,40,128]{2,1,0:T(8,128)(2,1)} %all-to-all-done.data_ref.rate_ref, bf16[32,40,128]{2,1,0:T(8,128)(2,1)} %all-to-all-done.data_ref.rate_ref, bf16[64,128,128]{2,1,0:T(8,128)(2,1)S(1)} %bitcast.17, f32[16,256]{1,0:T(8,128)S(1)} %pad.4.place_ref), custom_call_target="tpu_custom_call" | custom-call | tf_op jit(solution)/shard_map/grid_windows/pallas_call | solution.py:172
  25.6 1.6 %collective-permute-start.1 = (bf16[272,512]{1,0:T(8,128)(2,1)}, bf16[272,512]{1,0:T(8,128)(2,1)S(1)}, u32[]{:S(2)}, u32[]{:S(2)}) collective-permute-start(bf16[272,512]{1,0:T(8,128)(2,1)} %grid_windows.1.mine_ref.mine_notes), channel_id=1, source_target_pairs={{2,0},{3,1},{0,2},{1,3},{6,4},{7,5},{4,6},{5,7},{10,8},{11,9},{8,1... | collective-permute-start | bytes 835592 | tf_op jit(solution)/shard_map/ppermute | solution.py:400
  27.3 1.4 %collective-permute-start = (bf16[272,512]{1,0:T(8,128)(2,1)}, bf16[272,512]{1,0:T(8,128)(2,1)S(1)}, u32[]{:S(2)}, u32[]{:S(2)}) collective-permute-start(bf16[272,512]{1,0:T(8,128)(2,1)} %grid_windows.1.mine_ref.mine_notes), channel_id=1, source_target_pairs={{1,0},{0,1},{3,2},{2,3},{5,4},{4,5},{7,6},{6,7},{9,8},{8,9},{11,10... | collective-permute-start | bytes 835592 | tf_op jit(solution)/shard_map/ppermute | solution.py:400
  28.6 12.4 %collective-permute-done.3.mine_ref.mine_notes = bf16[272,512]{1,0:T(8,128)(2,1)S(1)} collective-permute-done((bf16[272,512]{1,0:T(8,128)(2,1)}, bf16[272,512]{1,0:T(8,128)(2,1)S(1)}, u32[]{:S(2)}, u32[]{:S(2)}) %collective-permute-start.3) | collective-permute-done | bytes 278560 | tf_op jit(solution)/shard_map/ppermute | solution.py:400
  41.7 1.3 %collective-permute-start.2 = (bf16[272,512]{1,0:T(8,128)(2,1)S(1)}, bf16[272,512]{1,0:T(8,128)(2,1)S(1)}, u32[]{:S(2)}, u32[]{:S(2)}) collective-permute-start(bf16[272,512]{1,0:T(8,128)(2,1)S(1)} %collective-permute-done.1.mine_ref.mine_notes), channel_id=1, source_target_pairs={{1,0},{0,1},{3,2},{2,3},{5,4},{4,5},{7,6},{6,7},{9,8},{8,9},{11,10... | collective-permute-start | bytes 835592 | tf_op jit(solution)/shard_map/ppermute | solution.py:400
  44.0 2.3 %transform_columns.4 = (bf16[2,1280,256]{2,1,0:T(8,128)(2,1)S(1)}, bf16[2,16,256]{2,1,0:T(8,128)(2,1)S(1)}) custom-call(s32[1]{0:T(128)} %bitcast.odd_ref, bf16[272,512]{1,0:T(8,128)(2,1)} %grid_windows.1.mine_ref.mine_notes, bf16[272,512]{1,0:T(8,128)(2,1)} %grid_windows.1.mine_ref.mine_notes, ...), custom_call_target="tpu_custom_call" | custom-call | flops 671088640 | bytes 1310720 | tf_op jit(solution)/shard_map/transform_columns/pallas_call | solution.py:225
  46.3 1.9 %expand_rows.6.refs_0_ = bf16[160,5,16,128]{3,2,1,0:T(8,128)(2,1)S(1)} custom-call(bf16[2,1280,256]{2,1,0:T(8,128)(2,1)S(1)} %get-tuple-element.26.refs_0_.refs_1_, bf16[2,1280,256]{2,1,0:T(8,128)(2,1)S(1)} %get-tuple-element.26.refs_0_.refs_1_, bf16[2,16,256]{2,1,0:T(8,128)(2,1)S(1)} %get-tuple-element.27.refs_2_.refs_3_, ...), custom_call_target="tpu_custom_call" | custom-call | flops 1677721600 | bytes 3276800 | tf_op jit(solution)/shard_map/expand_rows/pallas_call | solution.py:311
  48.9 1.4 %collective-permute-start.6 = (bf16[272,512]{1,0:T(8,128)(2,1)S(1)}, bf16[272,512]{1,0:T(8,128)(2,1)S(1)}, u32[]{:S(2)}, u32[]{:S(2)}) collective-permute-start(bf16[272,512]{1,0:T(8,128)(2,1)S(1)} %collective-permute-done.5.mine_ref.mine_notes), channel_id=1, source_target_pairs={{1,0},{0,1},{3,2},{2,3},{5,4},{4,5},{7,6},{6,7},{9,8},{8,9},{11,10... | collective-permute-start | bytes 835592 | tf_op jit(solution)/shard_map/ppermute | solution.py:400
  50.6 1.4 %transform_columns.6 = (bf16[2,1280,256]{2,1,0:T(8,128)(2,1)S(1)}, bf16[2,16,256]{2,1,0:T(8,128)(2,1)S(1)}) custom-call(s32[1]{0:T(128)} %bitcast.odd_ref, bf16[272,512]{1,0:T(8,128)(2,1)S(1)} %collective-permute-done.3.mine_ref.mine_notes, bf16[272,512]{1,0:T(8,128)(2,1)S(1)} %collective-permute-done.3.mine_ref.mine_notes, ...), custom_call_target="tpu_custom_call" | custom-call | flops 671088640 | bytes 1310720 | tf_op jit(solution)/shard_map/transform_columns/pallas_call | solution.py:225
  51.9 1.9 %expand_rows.9.refs_3_ = bf16[160,5,16,128]{3,2,1,0:T(8,128)(2,1)S(1)} custom-call(bf16[2,1280,256]{2,1,0:T(8,128)(2,1)S(1)} %get-tuple-element.30.refs_1_.refs_0_, bf16[2,1280,256]{2,1,0:T(8,128)(2,1)S(1)} %get-tuple-element.30.refs_1_.refs_0_, bf16[2,16,256]{2,1,0:T(8,128)(2,1)S(1)} %get-tuple-element.31.refs_3_.refs_2_, ...), custom_call_target="tpu_custom_call" | custom-call | flops 1677721600 | bytes 3276800 | tf_op jit(solution)/shard_map/expand_rows/pallas_call | solution.py:311
  53.9 2.7 %collective-permute-done.2.other_ref.other_notes = bf16[272,512]{1,0:T(8,128)(2,1)S(1)} collective-permute-done((bf16[272,512]{1,0:T(8,128)(2,1)S(1)}, bf16[272,512]{1,0:T(8,128)(2,1)S(1)}, u32[]{:S(2)}, u32[]{:S(2)}) %collective-permute-start.2) | collective-permute-done | bytes 278560 | tf_op jit(solution)/shard_map/ppermute | solution.py:400
  56.5 1.4 %transform_columns.5 = (bf16[2,1280,256]{2,1,0:T(8,128)(2,1)S(1)}, bf16[2,16,256]{2,1,0:T(8,128)(2,1)S(1)}) custom-call(s32[1]{0:T(128)} %bitcast.odd_ref, bf16[272,512]{1,0:T(8,128)(2,1)S(1)} %collective-permute-done.1.mine_ref.mine_notes, bf16[272,512]{1,0:T(8,128)(2,1)S(1)} %collective-permute-done.1.mine_ref.mine_notes, ...), custom_call_target="tpu_custom_call" | custom-call | flops 671088640 | bytes 1310720 | tf_op jit(solution)/shard_map/transform_columns/pallas_call | solution.py:225
  57.9 1.9 %expand_rows.8.refs_2_ = bf16[160,5,16,128]{3,2,1,0:T(8,128)(2,1)S(1)} custom-call(bf16[2,1280,256]{2,1,0:T(8,128)(2,1)S(1)} %get-tuple-element.28.refs_1_.refs_0_, bf16[2,1280,256]{2,1,0:T(8,128)(2,1)S(1)} %get-tuple-element.30.refs_1_.refs_0_, bf16[2,16,256]{2,1,0:T(8,128)(2,1)S(1)} %get-tuple-element.29.refs_3_.refs_2_, ...), custom_call_target="tpu_custom_call" | custom-call | flops 1677721600 | bytes 3276800 | tf_op jit(solution)/shard_map/expand_rows/pallas_call | solution.py:311
  59.8 1.9 %expand_rows.7.refs_1_ = bf16[160,5,16,128]{3,2,1,0:T(8,128)(2,1)S(1)} custom-call(bf16[2,1280,256]{2,1,0:T(8,128)(2,1)S(1)} %get-tuple-element.26.refs_0_.refs_1_, bf16[2,1280,256]{2,1,0:T(8,128)(2,1)S(1)} %get-tuple-element.28.refs_1_.refs_0_, bf16[2,16,256]{2,1,0:T(8,128)(2,1)S(1)} %get-tuple-element.27.refs_2_.refs_3_, ...), custom_call_target="tpu_custom_call" | custom-call | flops 1677721600 | bytes 3276800 | tf_op jit(solution)/shard_map/expand_rows/pallas_call | solution.py:311
  61.7 1.6 %transform_columns.7 = (bf16[2,1280,256]{2,1,0:T(8,128)(2,1)S(1)}, bf16[2,16,256]{2,1,0:T(8,128)(2,1)S(1)}) custom-call(s32[1]{0:T(128)} %bitcast.odd_ref, bf16[272,512]{1,0:T(8,128)(2,1)S(1)} %collective-permute-done.5.mine_ref.mine_notes, bf16[272,512]{1,0:T(8,128)(2,1)S(1)} %collective-permute-done.5.mine_ref.mine_notes, ...), custom_call_target="tpu_custom_call" | custom-call | flops 671088640 | bytes 1310720 | tf_op jit(solution)/shard_map/transform_columns/pallas_call | solution.py:225
  63.3 1.1 %expand_rows.11.refs_5_ = bf16[160,5,16,128]{3,2,1,0:T(8,128)(2,1)S(1)} custom-call(bf16[2,1280,256]{2,1,0:T(8,128)(2,1)S(1)} %get-tuple-element.32.refs_0_, bf16[2,16,256]{2,1,0:T(8,128)(2,1)S(1)} %get-tuple-element.33.refs_1_), custom_call_target="tpu_custom_call" | custom-call | flops 838860800 | bytes 3276800 | tf_op jit(solution)/shard_map/expand_rows/pallas_call | solution.py:311
  64.4 1.1 %expand_rows.10.refs_4_ = bf16[160,5,16,128]{3,2,1,0:T(8,128)(2,1)S(1)} custom-call(bf16[2,1280,256]{2,1,0:T(8,128)(2,1)S(1)} %get-tuple-element.32.refs_0_, bf16[2,16,256]{2,1,0:T(8,128)(2,1)S(1)} %get-tuple-element.33.refs_1_), custom_call_target="tpu_custom_call" | custom-call | flops 838860800 | bytes 3276800 | tf_op jit(solution)/shard_map/expand_rows/pallas_call | solution.py:311
  65.6 16.6 %form_image.1 = bf16[640,12800]{1,0:T(8,128)(2,1)} custom-call(bf16[160,5,16,128]{3,2,1,0:T(8,128)(2,1)S(1)} %expand_rows.6.refs_0_, bf16[160,5,16,128]{3,2,1,0:T(8,128)(2,1)S(1)} %expand_rows.7.refs_1_, bf16[160,5,16,128]{3,2,1,0:T(8,128)(2,1)S(1)} %expand_rows.8.refs_2_, bf16[160,5,16,128]{3,2,1,0:T(8,128)(2,1)S(1)} %expand_rows.9.refs_3_, ...), custom_call_target="tpu_custom_call" | custom-call | flops 12582912000 | bytes 32768000 | tf_op jit(solution)/shard_map/form_image/pallas_call | solution.py:356
  (39 shorter events, 7.3 us)
Async XLA Ops:
  0.0 14.7 %copy-start.3 = (bf16[640,1280]{1,0:T(8,128)(2,1)S(1)}, bf16[640,1280]{1,0:T(8,128)(2,1)}, u32[]{:S(2)}) copy-start(bf16[640,1280]{1,0:T(8,128)(2,1)} %constant.112.clone.wave_ref) | copy-start | bytes 4915204
  2.2 19.5 %all-to-all-start = ((bf16[32,40,128]{2,1,0:T(8,128)(2,1)}), bf16[32,40,128]{2,1,0:T(8,128)(2,1)}, u32[]{:S(2)}, u32[]{:S(2)}) async-start(bf16[32,40,128]{2,1,0:T(8,128)(2,1)} %pack_slots.1), calls=%async_computation | async-start | bytes 655360 | tf_op jit(solution)/shard_map/all_to_all | solution.py:420
  13.9 2.4 %copy-start = (bf16[80,1280]{1,0:T(8,128)(2,1)}, bf16[80,1280]{1,0:T(8,128)(2,1)S(1)}, u32[]{:S(2)}) copy-start(bf16[80,1280]{1,0:T(8,128)(2,1)S(1)} %constant_dynamic-slice_fusion.rows_ref.wave_ref) | copy-start | bytes 614404
  16.2 0.9 %copy-start.4 = (bf16[2,320,768]{2,1,0:T(8,128)(2,1)}, bf16[2,320,768]{2,1,0:T(8,128)(2,1)S(1)}, u32[]{:S(2)}) copy-start(bf16[2,320,768]{2,1,0:T(8,128)(2,1)S(1)} %get-tuple-element.34.refs_6_) | copy-start | bytes 2949124
  25.6 15.4 %collective-permute-start.3 = (bf16[272,512]{1,0:T(8,128)(2,1)}, bf16[272,512]{1,0:T(8,128)(2,1)S(1)}, u32[]{:S(2)}, u32[]{:S(2)}) collective-permute-start(bf16[272,512]{1,0:T(8,128)(2,1)} %grid_windows.1.mine_ref.mine_notes), channel_id=1, source_target_pairs={{4,0},{5,1},{6,2},{7,3},{0,4},{1,5},{2,6},{3,7},{12,8},{13,9},{14,... | collective-permute-start | bytes 835592 | tf_op jit(solution)/shard_map/ppermute | solution.py:400
  25.6 16.1 %collective-permute-start.1 = (bf16[272,512]{1,0:T(8,128)(2,1)}, bf16[272,512]{1,0:T(8,128)(2,1)S(1)}, u32[]{:S(2)}, u32[]{:S(2)}) collective-permute-start(bf16[272,512]{1,0:T(8,128)(2,1)} %grid_windows.1.mine_ref.mine_notes), channel_id=1, source_target_pairs={{2,0},{3,1},{0,2},{1,3},{6,4},{7,5},{4,6},{5,7},{10,8},{11,9},{8,1... | collective-permute-start | bytes 835592 | tf_op jit(solution)/shard_map/ppermute | solution.py:400
  27.3 15.8 %collective-permute-start = (bf16[272,512]{1,0:T(8,128)(2,1)}, bf16[272,512]{1,0:T(8,128)(2,1)S(1)}, u32[]{:S(2)}, u32[]{:S(2)}) collective-permute-start(bf16[272,512]{1,0:T(8,128)(2,1)} %grid_windows.1.mine_ref.mine_notes), channel_id=1, source_target_pairs={{1,0},{0,1},{3,2},{2,3},{5,4},{4,5},{7,6},{6,7},{9,8},{8,9},{11,10... | collective-permute-start | bytes 835592 | tf_op jit(solution)/shard_map/ppermute | solution.py:400
  41.0 7.9 %collective-permute-start.5 = (bf16[272,512]{1,0:T(8,128)(2,1)S(1)}, bf16[272,512]{1,0:T(8,128)(2,1)S(1)}, u32[]{:S(2)}, u32[]{:S(2)}) collective-permute-start(bf16[272,512]{1,0:T(8,128)(2,1)S(1)} %collective-permute-done.3.mine_ref.mine_notes), channel_id=1, source_target_pairs={{2,0},{3,1},{0,2},{1,3},{6,4},{7,5},{4,6},{5,7},{10,8},{11,9},{8,1... | collective-permute-start | bytes 835592 | tf_op jit(solution)/shard_map/ppermute | solution.py:400
  41.0 9.5 %collective-permute-start.4 = (bf16[272,512]{1,0:T(8,128)(2,1)S(1)}, bf16[272,512]{1,0:T(8,128)(2,1)S(1)}, u32[]{:S(2)}, u32[]{:S(2)}) collective-permute-start(bf16[272,512]{1,0:T(8,128)(2,1)S(1)} %collective-permute-done.3.mine_ref.mine_notes), channel_id=1, source_target_pairs={{1,0},{0,1},{3,2},{2,3},{5,4},{4,5},{7,6},{6,7},{9,8},{8,9},{11,10... | collective-permute-start | bytes 835592 | tf_op jit(solution)/shard_map/ppermute | solution.py:400
  41.7 14.8 %collective-permute-start.2 = (bf16[272,512]{1,0:T(8,128)(2,1)S(1)}, bf16[272,512]{1,0:T(8,128)(2,1)S(1)}, u32[]{:S(2)}, u32[]{:S(2)}) collective-permute-start(bf16[272,512]{1,0:T(8,128)(2,1)S(1)} %collective-permute-done.1.mine_ref.mine_notes), channel_id=1, source_target_pairs={{1,0},{0,1},{3,2},{2,3},{5,4},{4,5},{7,6},{6,7},{9,8},{8,9},{11,10... | collective-permute-start | bytes 835592 | tf_op jit(solution)/shard_map/ppermute | solution.py:400
  43.1 0.9 %copy-start.1 = (bf16[80,1280]{1,0:T(8,128)(2,1)S(1)}, bf16[80,1280]{1,0:T(8,128)(2,1)}, u32[]{:S(2)}) copy-start(bf16[80,1280]{1,0:T(8,128)(2,1)} %copy-done) | copy-start | bytes 614404
  46.3 4.2 %copy-start.2 = (bf16[80,1280]{1,0:T(8,128)(2,1)S(1)}, bf16[80,1280]{1,0:T(8,128)(2,1)}, u32[]{:S(2)}) copy-start(bf16[80,1280]{1,0:T(8,128)(2,1)} %copy-done) | copy-start | bytes 614404
  48.9 12.8 %collective-permute-start.6 = (bf16[272,512]{1,0:T(8,128)(2,1)S(1)}, bf16[272,512]{1,0:T(8,128)(2,1)S(1)}, u32[]{:S(2)}, u32[]{:S(2)}) collective-permute-start(bf16[272,512]{1,0:T(8,128)(2,1)S(1)} %collective-permute-done.5.mine_ref.mine_notes), channel_id=1, source_target_pairs={{1,0},{0,1},{3,2},{2,3},{5,4},{4,5},{7,6},{6,7},{9,8},{8,9},{11,10... | collective-permute-start | bytes 835592 | tf_op jit(solution)/shard_map/ppermute | solution.py:400
  64.4 1.2 %copy-start.5 = (bf16[2,320,768]{2,1,0:T(8,128)(2,1)S(1)}, bf16[2,320,768]{2,1,0:T(8,128)(2,1)}, u32[]{:S(2)}) copy-start(bf16[2,320,768]{2,1,0:T(8,128)(2,1)} %copy-done.4) | copy-start | bytes 2949124
where the time goes:
time: 82.7 us; the launch traced here: 82.2 us
  Pallas kernels  40.5 us (49%)
  waiting for transfers between devices  19.8 us (24%)
  starting transfers between devices  13.9 us (17%)
  local copies, waits for them, and re-layouts  4.76 us (6%)
  other arithmetic  2.87 us (3%)
    pallas_call x1, Pallas kernels, form_image(): pl.pallas_call(image_kernel, grid=(groups // step,), in_specs=[*(pl.Block...  16.6 us
    ppermute x7, waiting for transfers between devices, from_tiles(): lax.ppermute(value, 'tile', [(source_of(t), t) for t in range(count)])  16 us
    pallas_call x6, Pallas kernels, expand_rows(): pl.pallas_call(functools.partial(rows_kernel, seats, second, ranks, coils...  9.75 us
    all_to_all x1, starting transfers between devices, body(): lax.all_to_all(packed, ('kz', 'tile'), split_axis=0, concat_axis=0, tiled...  7.44 us
    pallas_call x4, Pallas kernels, transform_columns(): pl.pallas_call(functools.partial(columns_kernel, coils), grid=(2, per), i...  6.62 us
    ppermute x7, starting transfers between devices, from_tiles(): lax.ppermute(value, 'tile', [(source_of(t), t) for t in range(count)])  6.46 us
    pallas_call x1, Pallas kernels, grid_windows(): pl.pallas_call(functools.partial(window_kernel, slots, pair), grid=(devic...  3.93 us
    all_to_all x1, waiting for transfers between devices, body(): lax.all_to_all(packed, ('kz', 'tile'), split_axis=0, concat_axis=0, tiled...  3.86 us
  transfers between devices with their start and end apart: 8, of which 5 were waited for; matrix products, arithmetic and copies ran while one was open for 7% of the time, Pallas kernels for 17%

commit v1 on v0

--- a/solution.py
+++ b/solution.py
@@ -250,7 +250,7 @@
     )(odd, mine, mine, other, other, table, wave_rows)
 
 
-def rows_kernel(seats, second, ranks, coils, *refs):
+def rows_kernel(seats, second, mirror, ranks, coils, *refs):
     near = len(seats)
     mids = refs[:near]
     notes = refs[near : 2 * near]
@@ -263,9 +263,12 @@
     half = LANES // 2
     lane = lax.broadcasted_iota(jnp.int32, (LANES, chunk), 0)
     odd = (lane >= half) if not second else (lane < half)
-    spot = (2 * (lane % half + half * second) + odd.astype(jnp.int32)).astype(jnp.float32)
+    spot = (2 * (lane % half) + odd.astype(jnp.int32)).astype(jnp.float32)
     told = [note[0].astype(jnp.float32) for note in notes]
-    hits = [told[d][ROW_NOTE : ROW_NOTE + 1] + 2.0 * seats[d] == spot for d in range(near)]
+    rows_told = [note[ROW_NOTE : ROW_NOTE + 1] for note in told]
+    if mirror is not None:
+        rows_told = [mirror - note for note in rows_told]
+    hits = [rows_told[d] + 2.0 * seats[d] == spot for d in range(near)]
 
     def finish(pair, total):
         low = total[:, :LANES].reshape(groups, 1, coils, LANES)
@@ -301,7 +304,7 @@
                 finish(pair, held[pair])
 
 
-def expand_rows(mids, notes, picks, seats, second, ranks, coils):
+def expand_rows(mids, notes, picks, seats, second, mirror, ranks, coils):
     _, rows, depth = mids[0].shape
     near = len(mids)
     chunk = min(depth, CHUNK)
@@ -309,7 +312,7 @@
     groups = rows // coils
     shape = (groups, ranks // 2, 2 * coils, LANES)
     return pl.pallas_call(
-        functools.partial(rows_kernel, seats, second, ranks, coils),
+        functools.partial(rows_kernel, seats, second, mirror, ranks, coils),
         grid=(per,),
         in_specs=[
             *(pl.BlockSpec((1, rows, chunk), lambda k, e=e: (e, 0, k)) for e in picks),
@@ -326,38 +329,41 @@
     )(*mids, *notes)
 
 
-def image_kernel(*refs):
+def image_kernel(count, *refs):
     waves_ref, out_ref = refs[-2:]
     plane = out_ref.shape[0]
     half = plane // 2
-    firsts = [ref[...] for ref in refs[:-2:2]]
-    seconds = [ref[...] for ref in refs[1:-2:2]]
-    groups, pairs, inner, _ = firsts[0].shape
+    groups, pairs, inner, _ = refs[0].shape
     columns = groups * pairs * inner
-    lower = lax.broadcasted_iota(jnp.int32, firsts[0].shape, 3) < LANES // 2
-    sums = []
+    sums, turns = [], []
+    for direct, mirrored in zip(refs[:count], refs[count : 2 * count]):
+        ahead, behind = direct[...], mirrored[...]
+        sums.append(ahead + behind)
+        gap = (ahead - behind).reshape(groups // 2, 2, pairs, inner, LANES)
+        turns.append(jnp.concatenate([-gap[:, 1:2], gap[:, 0:1]], axis=1).reshape(ahead.shape))
+    lower = lax.broadcasted_iota(jnp.int32, refs[0].shape, 3) < LANES // 2
+    halves = []
     for parity in range(2):
-        chosen = zip(firsts, seconds) if parity == 0 else zip(seconds, firsts)
-        block = jnp.concatenate([jnp.where(lower, a, b) for a, b in chosen], axis=-1)
-        lanes = block.shape[-1]
-        block = block.reshape(groups // 2, 2, pairs * inner, lanes)
-        crossed = jnp.concatenate([-block[:, 1:2], block[:, 0:1]], axis=1)
-        right = jnp.concatenate([block.reshape(columns, lanes), crossed.reshape(columns, lanes)], axis=1)
-        sums.append(dot_nt(waves_ref[parity], right))
-    out_ref[:half, :] = ((sums[0] + sums[1]) * (1.0 / plane)).astype(jnp.bfloat16)
-    out_ref[half:, :] = ((sums[0] - sums[1]) * (1.0 / plane)).astype(jnp.bfloat16)
-
-
-def form_image(blocks, waves):
+        chosen = [
+            jnp.where(lower, part[n + parity], part[n + 1 - parity]).reshape(columns, LANES)
+            for part in (sums, turns)
+            for n in range(0, count, 2)
+        ]
+        halves.append(dot_nt(waves_ref[parity], jnp.concatenate(chosen, axis=1)))
+    out_ref[:half, :] = ((halves[0] + halves[1]) * (1.0 / plane)).astype(jnp.bfloat16)
+    out_ref[half:, :] = ((halves[0] - halves[1]) * (1.0 / plane)).astype(jnp.bfloat16)
+
+
+def form_image(direct, mirrored, waves):
     plane = 2 * waves.shape[1]
-    groups, pairs, inner, _ = blocks[0].shape
+    groups, pairs, inner, _ = direct[0].shape
     step = next(n for n in (16, 8, 4, 2) if groups % n == 0)
     columns = step * pairs * inner
     return pl.pallas_call(
-        image_kernel,
+        functools.partial(image_kernel, len(direct)),
         grid=(groups // step,),
         in_specs=[
-            *(pl.BlockSpec((step, pairs, inner, LANES), lambda s: (s, 0, 0, 0)) for _ in blocks),
+            *(pl.BlockSpec((step, pairs, inner, LANES), lambda s: (s, 0, 0, 0)) for _ in (*direct, *mirrored)),
             pl.BlockSpec(waves.shape, lambda s: (0, 0, 0)),
         ],
         out_specs=pl.BlockSpec((plane, columns), lambda s: (0, s)),
@@ -369,29 +375,27 @@
             transcendentals=0,
         ),
         name="form_image",
-    )(*blocks, waves)
+    )(*direct, *mirrored, waves)
 
 
 def pack_tiles(tiles, tile_rows):
-    span = (tile_rows + WIN_ROWS) // 2
-    room = LANES // span
-    twos = []
-    for first in range(0, tiles, room):
-        members = list(range(first, min(first + room, tiles)))
-        stride = LANES // 2 if len(members) <= 2 and span <= LANES // 2 else span
-        twos.append([(t, n * stride) for n, t in enumerate(members)])
-    return twos, span
-
-
-def kx_of_lanes(twos, span):
-    at = np.full((2, 2, len(twos) * LANES), -1, np.int32)
-    for n, members in enumerate(twos):
+    span = (tile_rows + WIN_ROWS) // 2 + 1
+    room = LANES // 2 // span
+    blocks = []
+    for first in range(0, tiles // 2, room):
+        blocks.append([(t, n * span) for n, t in enumerate(range(first, min(first + room, tiles // 2)))])
+    return blocks + [[]] * (len(blocks) % 2), span
+
+
+def kx_of_lanes(blocks, span):
+    half = LANES // 2
+    at = np.full((2, 2, len(blocks) * half), -1, np.int32)
+    for n, members in enumerate(blocks):
         for t, seat in members:
             for k in range(span):
-                even = seat + k
-                odd = (seat + k + LANES // 2) % LANES
-                at[:, 0, n * LANES + even] = t, 2 * k
-                at[:, 1, n * LANES + odd] = t, 2 * k + 1
+                lane = n // 2 * LANES + seat + k
+                at[:, 0, lane + half * (n % 2)] = t, 2 * k
+                at[:, 1, lane + half * (1 - n % 2)] = t, 2 * k + 1
     return at
 
 
@@ -437,8 +441,8 @@
     cos_tab, sin_tab = wave_tables()
     wave = jnp.asarray(np.concatenate([cos_tab, sin_tab], axis=1))
     wave_rows = lax.dynamic_slice_in_dim(wave, my_tile * ys, ys, 0)
-    twos, span = pack_tiles(tiles, tile_rows)
-    arrival, window_row = (jnp.asarray(part) for part in kx_of_lanes(twos, span))
+    layout, span = pack_tiles(tiles, tile_rows)
+    arrival, window_row = (jnp.asarray(part) for part in kx_of_lanes(layout, span))
     lane_tile = (arrival // 2 ^ my_tile // 2) * 2 + arrival % 2
     lane_rows = jnp.where(arrival < 0, -1, (lane_tile * tile_rows - 2 + window_row + PLANE) % PLANE)
     table, waves = make_tables(wave, wave_rows, lane_rows, coils)
@@ -460,22 +464,22 @@
         mids.append(mid)
         notes.append(note)
 
-    blocks = []
-    for members in twos:
-        for second in range(2):
-            low, high = second * (LANES // 2), (second + 1) * (LANES // 2)
-            met = [(t, seat) for t, seat in members if seat < high and seat + span > low]
+    direct, mirrored = [], []
+    for n, members in enumerate(layout):
+        for mirror, blocks in ((None, direct), (float(tile_rows + WIN_ROWS), mirrored)):
+            met = [(t if mirror is None else t ^ (tiles - 1), seat) for t, seat in members]
             block = expand_rows(
                 [mids[t // 2] for t, _ in met],
                 [notes[t // 2] for t, _ in met],
                 [t % 2 for t, _ in met],
                 [float(seat) for _, seat in met],
-                second,
+                n % 2,
+                mirror,
                 ranks,
                 coils,
-            )
+            ) if met else jnp.zeros_like(blocks[0])
             blocks.append(block)
-    return form_image(blocks, waves)[None]
+    return form_image(direct, mirrored, waves)[None]
 
 
 def solution(mesh):

time: 82.7 us -> 80.6 us (0.975)
  Pallas kernels: 40.5 us -> 37.3 us
  waiting for transfers between devices: 19.8 us -> 21.1 us
    pallas_call x7 -> x9, Pallas kernels: 26.3 us -> 23.6 us  [the longest x1 15.2 us: form_image(): pl.pallas_call(functools.partial(image_kernel, len(direct)), grid=(groups...]
  transfers between devices with their start and end apart: 8 -> 8, of which waited for: 5 -> 5; matrix products, arithmetic and copies ran while one was open for 7% -> 7% of each run, Pallas kernels for 17% -> 15%
where the time goes in v1:
time: 80.6 us; the launch traced here: 80 us
  Pallas kernels  37.3 us (46%)
  waiting for transfers between devices  21.1 us (26%)
  starting transfers between devices  13.9 us (17%)
  local copies, waits for them, and re-layouts  4.53 us (6%)
  other arithmetic  2.86 us (4%)
    ppermute x7, waiting for transfers between devices, from_tiles(): lax.ppermute(value, 'tile', [(source_of(t), t) for t in range(count)])  16.6 us
    pallas_call x1, Pallas kernels, form_image(): pl.pallas_call(functools.partial(image_kernel, len(direct)), grid=(groups...  15.2 us
    pallas_call x8, Pallas kernels, expand_rows(): pl.pallas_call(functools.partial(rows_kernel, seats, second, mirror, rank...  8.43 us
    all_to_all x1, starting transfers between devices, body(): lax.all_to_all(packed, ('kz', 'tile'), split_axis=0, concat_axis=0, tiled...  7.44 us
    pallas_call x4, Pallas kernels, transform_columns(): pl.pallas_call(functools.partial(columns_kernel, coils), grid=(2, per), i...  6.62 us
    ppermute x7, starting transfers between devices, from_tiles(): lax.ppermute(value, 'tile', [(source_of(t), t) for t in range(count)])  6.46 us
    all_to_all x1, waiting for transfers between devices, body(): lax.all_to_all(packed, ('kz', 'tile'), split_axis=0, concat_axis=0, tiled...  4.49 us
    pallas_call x1, Pallas kernels, grid_windows(): pl.pallas_call(functools.partial(window_kernel, slots, pair), grid=(devic...  3.93 us
  transfers between devices with their start and end apart: 8, of which 5 were waited for; matrix products, arithmetic and copies ran while one was open for 7% of the time, Pallas kernels for 15%

profile of v1, /device:TPU:0, one launch (start us, length us, event | category | flops | bytes accessed | tf_op | source)
XLA Modules:
  0.0 80.0 jit_solution(18175243559867554371)
XLA Ops:
  0.0 2.2 %pack_slots.1 = bf16[32,40,128]{2,1,0:T(8,128)(2,1)} custom-call(s32[1,1,4,2,8]{4,3,2,1,0:T(2,128)} %bitcast.21, bf16[1,1,4,8,2,16,128]{6,5,4,3,2,1,0:T(8,128)(2,1)} %data_ref.1, bf16[10,1000]{1,0:T(8,128)(2,1)} %bitcast.20), custom_call_target="tpu_custom_call" | custom-call | tf_op jit(solution)/shard_map/pack_slots/pallas_call | solution.py:112
  2.2 7.4 %all-to-all-start = ((bf16[32,40,128]{2,1,0:T(8,128)(2,1)}), bf16[32,40,128]{2,1,0:T(8,128)(2,1)}, u32[]{:S(2)}, u32[]{:S(2)}) async-start(bf16[32,40,128]{2,1,0:T(8,128)(2,1)} %pack_slots.1), calls=%async_computation | async-start | bytes 655360 | tf_op jit(solution)/shard_map/all_to_all | solution.py:424
  11.8 1.0 %bitcast_select_fusion = f32[64,2,128]{2,1,0:T(2,128)S(1)} fusion(f32[1,1,4,8,2,2,128]{6,5,4,3,2,1,0:T(2,128)} %param.12, pred[64]{0:T(512)(128)(4,1)S(1)} %lt.60), kind=kLoop, calls=%fused_computation.3 | loop fusion | flops 16384 | bytes 131136 | tf_op jit(solution)/shard_map/jit(_where)/select_n | solution.py:429
  17.2 4.5 %all-to-all-done.data_ref.rate_ref = bf16[32,40,128]{2,1,0:T(8,128)(2,1)} async-done(((bf16[32,40,128]{2,1,0:T(8,128)(2,1)}), bf16[32,40,128]{2,1,0:T(8,128)(2,1)}, u32[]{:S(2)}, u32[]{:S(2)}) %all-to-all-start) | async-done | bytes 327712 | tf_op jit(solution)/shard_map/all_to_all | solution.py:424
  21.7 3.9 %grid_windows.1.mine_ref.mine_notes = bf16[272,512]{1,0:T(8,128)(2,1)} custom-call(bf16[32,40,128]{2,1,0:T(8,128)(2,1)} %all-to-all-done.data_ref.rate_ref, bf16[32,40,128]{2,1,0:T(8,128)(2,1)} %all-to-all-done.data_ref.rate_ref, bf16[64,128,128]{2,1,0:T(8,128)(2,1)S(1)} %bitcast.17, f32[16,256]{1,0:T(8,128)S(1)} %pad.4.place_ref), custom_call_target="tpu_custom_call" | custom-call | tf_op jit(solution)/shard_map/grid_windows/pallas_call | solution.py:172
  25.6 1.6 %collective-permute-start.1 = (bf16[272,512]{1,0:T(8,128)(2,1)}, bf16[272,512]{1,0:T(8,128)(2,1)S(1)}, u32[]{:S(2)}, u32[]{:S(2)}) collective-permute-start(bf16[272,512]{1,0:T(8,128)(2,1)} %grid_windows.1.mine_ref.mine_notes), channel_id=1, source_target_pairs={{2,0},{3,1},{0,2},{1,3},{6,4},{7,5},{4,6},{5,7},{10,8},{11,9},{8,1... | collective-permute-start | bytes 835592 | tf_op jit(solution)/shard_map/ppermute | solution.py:404
  27.3 1.4 %collective-permute-start = (bf16[272,512]{1,0:T(8,128)(2,1)}, bf16[272,512]{1,0:T(8,128)(2,1)S(1)}, u32[]{:S(2)}, u32[]{:S(2)}) collective-permute-start(bf16[272,512]{1,0:T(8,128)(2,1)} %grid_windows.1.mine_ref.mine_notes), channel_id=1, source_target_pairs={{1,0},{0,1},{3,2},{2,3},{5,4},{4,5},{7,6},{6,7},{9,8},{8,9},{11,10... | collective-permute-start | bytes 835592 | tf_op jit(solution)/shard_map/ppermute | solution.py:404
  28.6 12.4 %collective-permute-done.3.mine_ref.mine_notes = bf16[272,512]{1,0:T(8,128)(2,1)S(1)} collective-permute-done((bf16[272,512]{1,0:T(8,128)(2,1)}, bf16[272,512]{1,0:T(8,128)(2,1)S(1)}, u32[]{:S(2)}, u32[]{:S(2)}) %collective-permute-start.3) | collective-permute-done | bytes 278560 | tf_op jit(solution)/shard_map/ppermute | solution.py:404
  41.7 1.3 %collective-permute-start.2 = (bf16[272,512]{1,0:T(8,128)(2,1)S(1)}, bf16[272,512]{1,0:T(8,128)(2,1)S(1)}, u32[]{:S(2)}, u32[]{:S(2)}) collective-permute-start(bf16[272,512]{1,0:T(8,128)(2,1)S(1)} %collective-permute-done.1.mine_ref.mine_notes), channel_id=1, source_target_pairs={{1,0},{0,1},{3,2},{2,3},{5,4},{4,5},{7,6},{6,7},{9,8},{8,9},{11,10... | collective-permute-start | bytes 835592 | tf_op jit(solution)/shard_map/ppermute | solution.py:404
  44.0 2.3 %transform_columns.4 = (bf16[2,1280,256]{2,1,0:T(8,128)(2,1)S(1)}, bf16[2,16,256]{2,1,0:T(8,128)(2,1)S(1)}) custom-call(s32[1]{0:T(128)} %bitcast.odd_ref, bf16[272,512]{1,0:T(8,128)(2,1)} %grid_windows.1.mine_ref.mine_notes, bf16[272,512]{1,0:T(8,128)(2,1)} %grid_windows.1.mine_ref.mine_notes, ...), custom_call_target="tpu_custom_call" | custom-call | flops 671088640 | bytes 1310720 | tf_op jit(solution)/shard_map/transform_columns/pallas_call | solution.py:225
  46.3 1.1 %expand_rows.9.refs_1_ = bf16[160,5,16,128]{3,2,1,0:T(8,128)(2,1)S(1)} custom-call(bf16[2,1280,256]{2,1,0:T(8,128)(2,1)S(1)} %get-tuple-element.26.refs_0_, bf16[2,16,256]{2,1,0:T(8,128)(2,1)S(1)} %get-tuple-element.27.refs_1_), custom_call_target="tpu_custom_call" | custom-call | flops 838860800 | bytes 3276800 | tf_op jit(solution)/shard_map/expand_rows/pallas_call | solution.py:314
  47.4 1.0 %expand_rows.8.refs_0_ = bf16[160,5,16,128]{3,2,1,0:T(8,128)(2,1)S(1)} custom-call(bf16[2,1280,256]{2,1,0:T(8,128)(2,1)S(1)} %get-tuple-element.26.refs_0_, bf16[2,16,256]{2,1,0:T(8,128)(2,1)S(1)} %get-tuple-element.27.refs_1_), custom_call_target="tpu_custom_call" | custom-call | flops 838860800 | bytes 3276800 | tf_op jit(solution)/shard_map/expand_rows/pallas_call | solution.py:314
  48.9 1.4 %collective-permute-start.5 = (bf16[272,512]{1,0:T(8,128)(2,1)S(1)}, bf16[272,512]{1,0:T(8,128)(2,1)S(1)}, u32[]{:S(2)}, u32[]{:S(2)}) collective-permute-start(bf16[272,512]{1,0:T(8,128)(2,1)S(1)} %collective-permute-done.4.mine_ref.mine_notes), channel_id=1, source_target_pairs={{1,0},{0,1},{3,2},{2,3},{5,4},{4,5},{7,6},{6,7},{9,8},{8,9},{11,10... | collective-permute-start | bytes 835592 | tf_op jit(solution)/shard_map/ppermute | solution.py:404
  50.6 1.4 %transform_columns.7 = (bf16[2,1280,256]{2,1,0:T(8,128)(2,1)S(1)}, bf16[2,16,256]{2,1,0:T(8,128)(2,1)S(1)}) custom-call(s32[1]{0:T(128)} %bitcast.odd_ref, bf16[272,512]{1,0:T(8,128)(2,1)S(1)} %collective-permute-done.3.mine_ref.mine_notes, bf16[272,512]{1,0:T(8,128)(2,1)S(1)} %collective-permute-done.3.mine_ref.mine_notes, ...), custom_call_target="tpu_custom_call" | custom-call | flops 671088640 | bytes 1310720 | tf_op jit(solution)/shard_map/transform_columns/pallas_call | solution.py:225
  51.9 1.1 %expand_rows.15.refs_7_ = bf16[160,5,16,128]{3,2,1,0:T(8,128)(2,1)S(1)} custom-call(bf16[2,1280,256]{2,1,0:T(8,128)(2,1)S(1)} %get-tuple-element.32.refs_0_, bf16[2,16,256]{2,1,0:T(8,128)(2,1)S(1)} %get-tuple-element.33.refs_1_), custom_call_target="tpu_custom_call" | custom-call | flops 838860800 | bytes 3276800 | tf_op jit(solution)/shard_map/expand_rows/pallas_call | solution.py:314
  53.0 3.5 %collective-permute-done.2.other_ref.other_notes = bf16[272,512]{1,0:T(8,128)(2,1)S(1)} collective-permute-done((bf16[272,512]{1,0:T(8,128)(2,1)S(1)}, bf16[272,512]{1,0:T(8,128)(2,1)S(1)}, u32[]{:S(2)}, u32[]{:S(2)}) %collective-permute-start.2) | collective-permute-done | bytes 278560 | tf_op jit(solution)/shard_map/ppermute | solution.py:404
  56.5 1.4 %transform_columns.5 = (bf16[2,1280,256]{2,1,0:T(8,128)(2,1)S(1)}, bf16[2,16,256]{2,1,0:T(8,128)(2,1)S(1)}) custom-call(s32[1]{0:T(128)} %bitcast.odd_ref, bf16[272,512]{1,0:T(8,128)(2,1)S(1)} %collective-permute-done.1.mine_ref.mine_notes, bf16[272,512]{1,0:T(8,128)(2,1)S(1)} %collective-permute-done.1.mine_ref.mine_notes, ...), custom_call_target="tpu_custom_call" | custom-call | flops 671088640 | bytes 1310720 | tf_op jit(solution)/shard_map/transform_columns/pallas_call | solution.py:225
  57.9 1.1 %expand_rows.14.refs_6_ = bf16[160,5,16,128]{3,2,1,0:T(8,128)(2,1)S(1)} custom-call(bf16[2,1280,256]{2,1,0:T(8,128)(2,1)S(1)} %get-tuple-element.32.refs_0_, bf16[2,16,256]{2,1,0:T(8,128)(2,1)S(1)} %get-tuple-element.33.refs_1_), custom_call_target="tpu_custom_call" | custom-call | flops 838860800 | bytes 3276800 | tf_op jit(solution)/shard_map/expand_rows/pallas_call | solution.py:314
  59.0 1.1 %expand_rows.11.refs_3_ = bf16[160,5,16,128]{3,2,1,0:T(8,128)(2,1)S(1)} custom-call(bf16[2,1280,256]{2,1,0:T(8,128)(2,1)S(1)} %get-tuple-element.28.refs_0_, bf16[2,16,256]{2,1,0:T(8,128)(2,1)S(1)} %get-tuple-element.29.refs_1_), custom_call_target="tpu_custom_call" | custom-call | flops 838860800 | bytes 3276800 | tf_op jit(solution)/shard_map/expand_rows/pallas_call | solution.py:314
  60.0 1.1 %expand_rows.10.refs_2_ = bf16[160,5,16,128]{3,2,1,0:T(8,128)(2,1)S(1)} custom-call(bf16[2,1280,256]{2,1,0:T(8,128)(2,1)S(1)} %get-tuple-element.28.refs_0_, bf16[2,16,256]{2,1,0:T(8,128)(2,1)S(1)} %get-tuple-element.29.refs_1_), custom_call_target="tpu_custom_call" | custom-call | flops 838860800 | bytes 3276800 | tf_op jit(solution)/shard_map/expand_rows/pallas_call | solution.py:314
  61.1 1.6 %transform_columns.6 = (bf16[2,1280,256]{2,1,0:T(8,128)(2,1)S(1)}, bf16[2,16,256]{2,1,0:T(8,128)(2,1)S(1)}) custom-call(s32[1]{0:T(128)} %bitcast.odd_ref, bf16[272,512]{1,0:T(8,128)(2,1)S(1)} %collective-permute-done.4.mine_ref.mine_notes, bf16[272,512]{1,0:T(8,128)(2,1)S(1)} %collective-permute-done.4.mine_ref.mine_notes, ...), custom_call_target="tpu_custom_call" | custom-call | flops 671088640 | bytes 1310720 | tf_op jit(solution)/shard_map/transform_columns/pallas_call | solution.py:225
  62.7 1.0 %expand_rows.13.refs_5_ = bf16[160,5,16,128]{3,2,1,0:T(8,128)(2,1)S(1)} custom-call(bf16[2,1280,256]{2,1,0:T(8,128)(2,1)S(1)} %get-tuple-element.30.refs_0_, bf16[2,16,256]{2,1,0:T(8,128)(2,1)S(1)} %get-tuple-element.31.refs_1_), custom_call_target="tpu_custom_call" | custom-call | flops 838860800 | bytes 3276800 | tf_op jit(solution)/shard_map/expand_rows/pallas_call | solution.py:314
  63.8 1.1 %expand_rows.12.refs_4_ = bf16[160,5,16,128]{3,2,1,0:T(8,128)(2,1)S(1)} custom-call(bf16[2,1280,256]{2,1,0:T(8,128)(2,1)S(1)} %get-tuple-element.30.refs_0_, bf16[2,16,256]{2,1,0:T(8,128)(2,1)S(1)} %get-tuple-element.31.refs_1_), custom_call_target="tpu_custom_call" | custom-call | flops 838860800 | bytes 3276800 | tf_op jit(solution)/shard_map/expand_rows/pallas_call | solution.py:314
  64.8 15.2 %form_image.1 = bf16[640,12800]{1,0:T(8,128)(2,1)} custom-call(bf16[160,5,16,128]{3,2,1,0:T(8,128)(2,1)S(1)} %expand_rows.8.refs_0_, bf16[160,5,16,128]{3,2,1,0:T(8,128)(2,1)S(1)} %expand_rows.9.refs_1_, bf16[160,5,16,128]{3,2,1,0:T(8,128)(2,1)S(1)} %expand_rows.10.refs_2_, bf16[160,5,16,128]{3,2,1,0:T(8,128)(2,1)S(1)} %expand_rows.11.refs_3_, ...), custom_call_target="tpu_custom_call" | custom-call | flops 8388608000 | bytes 32768000 | tf_op jit(solution)/shard_map/form_image/pallas_call | solution.py:362
  (41 shorter events, 8.8 us)
Async XLA Ops:
  0.0 14.7 %copy-start.3 = (bf16[640,1280]{1,0:T(8,128)(2,1)S(1)}, bf16[640,1280]{1,0:T(8,128)(2,1)}, u32[]{:S(2)}) copy-start(bf16[640,1280]{1,0:T(8,128)(2,1)} %constant.112.clone.wave_ref) | copy-start | bytes 4915204
  2.2 19.5 %all-to-all-start = ((bf16[32,40,128]{2,1,0:T(8,128)(2,1)}), bf16[32,40,128]{2,1,0:T(8,128)(2,1)}, u32[]{:S(2)}, u32[]{:S(2)}) async-start(bf16[32,40,128]{2,1,0:T(8,128)(2,1)} %pack_slots.1), calls=%async_computation | async-start | bytes 655360 | tf_op jit(solution)/shard_map/all_to_all | solution.py:424
  13.9 1.9 %copy-start = (bf16[80,1280]{1,0:T(8,128)(2,1)}, bf16[80,1280]{1,0:T(8,128)(2,1)S(1)}, u32[]{:S(2)}) copy-start(bf16[80,1280]{1,0:T(8,128)(2,1)S(1)} %constant_dynamic-slice_fusion.rows_ref.wave_ref) | copy-start | bytes 614404
  15.7 0.8 %copy-start.4 = (bf16[2,320,512]{2,1,0:T(8,128)(2,1)}, bf16[2,320,512]{2,1,0:T(8,128)(2,1)S(1)}, u32[]{:S(2)}) copy-start(bf16[2,320,512]{2,1,0:T(8,128)(2,1)S(1)} %get-tuple-element.34.refs_8_) | copy-start | bytes 1966084
  25.6 15.4 %collective-permute-start.3 = (bf16[272,512]{1,0:T(8,128)(2,1)}, bf16[272,512]{1,0:T(8,128)(2,1)S(1)}, u32[]{:S(2)}, u32[]{:S(2)}) collective-permute-start(bf16[272,512]{1,0:T(8,128)(2,1)} %grid_windows.1.mine_ref.mine_notes), channel_id=1, source_target_pairs={{4,0},{5,1},{6,2},{7,3},{0,4},{1,5},{2,6},{3,7},{12,8},{13,9},{14,... | collective-permute-start | bytes 835592 | tf_op jit(solution)/shard_map/ppermute | solution.py:404
  25.6 16.1 %collective-permute-start.1 = (bf16[272,512]{1,0:T(8,128)(2,1)}, bf16[272,512]{1,0:T(8,128)(2,1)S(1)}, u32[]{:S(2)}, u32[]{:S(2)}) collective-permute-start(bf16[272,512]{1,0:T(8,128)(2,1)} %grid_windows.1.mine_ref.mine_notes), channel_id=1, source_target_pairs={{2,0},{3,1},{0,2},{1,3},{6,4},{7,5},{4,6},{5,7},{10,8},{11,9},{8,1... | collective-permute-start | bytes 835592 | tf_op jit(solution)/shard_map/ppermute | solution.py:404
  27.3 15.8 %collective-permute-start = (bf16[272,512]{1,0:T(8,128)(2,1)}, bf16[272,512]{1,0:T(8,128)(2,1)S(1)}, u32[]{:S(2)}, u32[]{:S(2)}) collective-permute-start(bf16[272,512]{1,0:T(8,128)(2,1)} %grid_windows.1.mine_ref.mine_notes), channel_id=1, source_target_pairs={{1,0},{0,1},{3,2},{2,3},{5,4},{4,5},{7,6},{6,7},{9,8},{8,9},{11,10... | collective-permute-start | bytes 835592 | tf_op jit(solution)/shard_map/ppermute | solution.py:404
  41.0 7.9 %collective-permute-start.4 = (bf16[272,512]{1,0:T(8,128)(2,1)S(1)}, bf16[272,512]{1,0:T(8,128)(2,1)S(1)}, u32[]{:S(2)}, u32[]{:S(2)}) collective-permute-start(bf16[272,512]{1,0:T(8,128)(2,1)S(1)} %collective-permute-done.3.mine_ref.mine_notes), channel_id=1, source_target_pairs={{2,0},{3,1},{0,2},{1,3},{6,4},{7,5},{4,6},{5,7},{10,8},{11,9},{8,1... | collective-permute-start | bytes 835592 | tf_op jit(solution)/shard_map/ppermute | solution.py:404
  41.0 9.5 %collective-permute-start.6 = (bf16[272,512]{1,0:T(8,128)(2,1)S(1)}, bf16[272,512]{1,0:T(8,128)(2,1)S(1)}, u32[]{:S(2)}, u32[]{:S(2)}) collective-permute-start(bf16[272,512]{1,0:T(8,128)(2,1)S(1)} %collective-permute-done.3.mine_ref.mine_notes), channel_id=1, source_target_pairs={{1,0},{0,1},{3,2},{2,3},{5,4},{4,5},{7,6},{6,7},{9,8},{8,9},{11,10... | collective-permute-start | bytes 835592 | tf_op jit(solution)/shard_map/ppermute | solution.py:404
  41.7 14.8 %collective-permute-start.2 = (bf16[272,512]{1,0:T(8,128)(2,1)S(1)}, bf16[272,512]{1,0:T(8,128)(2,1)S(1)}, u32[]{:S(2)}, u32[]{:S(2)}) collective-permute-start(bf16[272,512]{1,0:T(8,128)(2,1)S(1)} %collective-permute-done.1.mine_ref.mine_notes), channel_id=1, source_target_pairs={{1,0},{0,1},{3,2},{2,3},{5,4},{4,5},{7,6},{6,7},{9,8},{8,9},{11,10... | collective-permute-start | bytes 835592 | tf_op jit(solution)/shard_map/ppermute | solution.py:404
  43.1 0.9 %copy-start.1 = (bf16[80,1280]{1,0:T(8,128)(2,1)S(1)}, bf16[80,1280]{1,0:T(8,128)(2,1)}, u32[]{:S(2)}) copy-start(bf16[80,1280]{1,0:T(8,128)(2,1)} %copy-done) | copy-start | bytes 614404
  47.4 3.2 %copy-start.2 = (bf16[80,1280]{1,0:T(8,128)(2,1)S(1)}, bf16[80,1280]{1,0:T(8,128)(2,1)}, u32[]{:S(2)}) copy-start(bf16[80,1280]{1,0:T(8,128)(2,1)} %copy-done) | copy-start | bytes 614404
  48.9 12.2 %collective-permute-start.5 = (bf16[272,512]{1,0:T(8,128)(2,1)S(1)}, bf16[272,512]{1,0:T(8,128)(2,1)S(1)}, u32[]{:S(2)}, u32[]{:S(2)}) collective-permute-start(bf16[272,512]{1,0:T(8,128)(2,1)S(1)} %collective-permute-done.4.mine_ref.mine_notes), channel_id=1, source_target_pairs={{1,0},{0,1},{3,2},{2,3},{5,4},{4,5},{7,6},{6,7},{9,8},{8,9},{11,10... | collective-permute-start | bytes 835592 | tf_op jit(solution)/shard_map/ppermute | solution.py:404
  63.7 1.1 %copy-start.5 = (bf16[2,320,512]{2,1,0:T(8,128)(2,1)S(1)}, bf16[2,320,512]{2,1,0:T(8,128)(2,1)}, u32[]{:S(2)}) copy-start(bf16[2,320,512]{2,1,0:T(8,128)(2,1)} %copy-done.4) | copy-start | bytes 1966084

commit v2 on v1

--- a/solution.py
+++ b/solution.py
@@ -81,7 +81,7 @@
             jax.ShapeDtypeStruct((ys * 2 * coils, WIN_COLS * 2 * coils), jnp.bfloat16),
             jax.ShapeDtypeStruct((2, plane // 2, 2 * lane_rows.shape[1]), jnp.bfloat16),
         ],
-        compiler_params=pltpu.CompilerParams(vmem_limit_bytes=40 << 20),
+        compiler_params=pltpu.CompilerParams(vmem_limit_bytes=10 << 20),
         name="make_tables",
     )(wave, wave_rows, lane_rows)
 
@@ -184,7 +184,7 @@
             pltpu.VMEM((count * pair, LANES), jnp.float32),
             pltpu.VMEM((devices * rate_rows, LANES), jnp.float32),
         ],
-        compiler_params=pltpu.CompilerParams(vmem_limit_bytes=24 << 20),
+        compiler_params=pltpu.CompilerParams(vmem_limit_bytes=12 << 20),
         name="grid_windows",
     )(raw, raw, weights, place)
 
@@ -242,7 +242,7 @@
             jax.ShapeDtypeStruct((2, rows, depth), jnp.bfloat16),
             jax.ShapeDtypeStruct((2, NOTES, depth), jnp.bfloat16),
         ],
-        compiler_params=pltpu.CompilerParams(vmem_limit_bytes=28 << 20),
+        compiler_params=pltpu.CompilerParams(vmem_limit_bytes=10 << 20),
         cost_estimate=pl.CostEstimate(
             flops=2 * 2 * rows * width * depth, bytes_accessed=2 * 2 * rows * depth, transcendentals=0
         ),
@@ -250,141 +250,148 @@
     )(odd, mine, mine, other, other, table, wave_rows)
 
 
-def rows_kernel(seats, second, mirror, ranks, coils, *refs):
-    near = len(seats)
-    mids = refs[:near]
-    notes = refs[near : 2 * near]
-    out_ref = refs[2 * near]
-    held = refs[2 * near + 1] if len(refs) > 2 * near + 1 else None
+def rows_kernel(blocks, mirror, ranks, coils, *refs):
+    spread = 1 + max(group for members in blocks for group, _, _ in members)
+    mids, notes, refs = refs[:spread], refs[spread : 2 * spread], refs[2 * spread :]
+    earlier, refs = (refs[:2], refs[2:]) if mirror is not None else ((), refs)
+    outs, held = (refs[:-1], refs[-1]) if len(refs) % 2 else (refs, None)
     _, rows, chunk = mids[0].shape
     groups = rows // coils
     step = pl.program_id(0)
-    left = jnp.concatenate([mid[0] for mid in mids], axis=1)
     half = LANES // 2
     lane = lax.broadcasted_iota(jnp.int32, (LANES, chunk), 0)
-    odd = (lane >= half) if not second else (lane < half)
-    spot = (2 * (lane % half) + odd.astype(jnp.int32)).astype(jnp.float32)
-    told = [note[0].astype(jnp.float32) for note in notes]
-    rows_told = [note[ROW_NOTE : ROW_NOTE + 1] for note in told]
-    if mirror is not None:
-        rows_told = [mirror - note for note in rows_told]
-    hits = [rows_told[d] + 2.0 * seats[d] == spot for d in range(near)]
-
-    def finish(pair, total):
-        low = total[:, :LANES].reshape(groups, 1, coils, LANES)
-        high = total[:, LANES:].reshape(groups, 1, coils, LANES)
-        both = jnp.concatenate([low, high], axis=1).reshape(groups, 2 * coils, LANES)
-        out_ref[:, pair] = both.astype(jnp.bfloat16)
+    lefts, hits, told = [], [], []
+    for second, members in enumerate(blocks):
+        lefts.append(jnp.concatenate([mids[group][e] for group, e, _ in members], axis=1))
+        told.append([notes[group][e].astype(jnp.float32) for group, e, _ in members])
+        odd = (lane >= half) if not second else (lane < half)
+        spot = (2 * (lane % half) + odd.astype(jnp.int32)).astype(jnp.float32)
+        at = [note[ROW_NOTE : ROW_NOTE + 1] for note in told[second]]
+        at = at if mirror is None else [mirror - row for row in at]
+        hits.append([row + 2.0 * seat == spot for row, (_, _, seat) in zip(at, members)])
+
+    def finish(pair, first, second):
+        lower = lax.broadcasted_iota(jnp.int32, (rows, LANES), 1) < half
+        done = []
+        for a, b in ((first, second), (second, first)):
+            sides = [
+                jnp.where(lower, a[:, side * LANES : (side + 1) * LANES], b[:, side * LANES : (side + 1) * LANES])
+                for side in range(2)
+            ]
+            sides = [side.reshape(groups, 1, coils, LANES) for side in sides]
+            done.append(jnp.concatenate(sides, axis=1).reshape(groups, 2 * coils, LANES))
+        for parity, block in enumerate(done):
+            if mirror is None:
+                outs[parity][:, pair] = block.astype(jnp.bfloat16)
+            else:
+                ahead = earlier[parity][:, pair].astype(jnp.float32)
+                outs[parity][:, pair] = (ahead + block).astype(jnp.bfloat16)
+                gap = (ahead - block).reshape(groups // 2, 2, 2 * coils, LANES)
+                gap = jnp.concatenate([-gap[:, 1:2], gap[:, 0:1]], axis=1)
+                outs[2 + parity][:, pair] = gap.reshape(groups, 2 * coils, LANES).astype(jnp.bfloat16)
 
     for pair in range(ranks // 2):
-        right = jnp.concatenate(
-            [
+        totals = []
+        for left, hit, note in zip(lefts, hits, told):
+            right = [
                 jnp.concatenate(
-                    [jnp.where(hits[d], told[d][rank : rank + 1], 0.0).astype(jnp.bfloat16) for d in range(near)], axis=1
+                    [jnp.where(h, n[rank : rank + 1], 0.0).astype(jnp.bfloat16) for h, n in zip(hit, note)], axis=1
                 )
                 for rank in (2 * pair, 2 * pair + 1)
-            ],
-            axis=0,
-        )
-        total = dot_nt(left, right)
+            ]
+            totals.append(dot_nt(left, jnp.concatenate(right, axis=0)))
         if held is None:
-            finish(pair, total)
+            finish(pair, *totals)
         else:
 
             @pl.when(step == 0)
-            def _(pair=pair, total=total):
-                held[pair] = total
+            def _(pair=pair, totals=totals):
+                for n in range(2):
+                    held[pair, n] = totals[n]
 
             @pl.when(step > 0)
-            def _(pair=pair, total=total):
-                held[pair] += total
+            def _(pair=pair, totals=totals):
+                for n in range(2):
+                    held[pair, n] += totals[n]
 
             @pl.when(step == pl.num_programs(0) - 1)
             def _(pair=pair):
-                finish(pair, held[pair])
-
-
-def expand_rows(mids, notes, picks, seats, second, mirror, ranks, coils):
+                finish(pair, held[pair, 0], held[pair, 1])
+
+
+def expand_rows(mids, notes, blocks, mirror, earlier, ranks, coils):
     _, rows, depth = mids[0].shape
-    near = len(mids)
     chunk = min(depth, CHUNK)
     per = depth // chunk
-    groups = rows // coils
-    shape = (groups, ranks // 2, 2 * coils, LANES)
+    shape = (rows // coils, ranks // 2, 2 * coils, LANES)
+    outs = 2 if mirror is None else 4
+    met = sum(len(members) for members in blocks)
+    once = pl.BlockSpec(shape, lambda k: (0, 0, 0, 0), pipeline_mode=pl.Buffered(1))
     return pl.pallas_call(
-        functools.partial(rows_kernel, seats, second, mirror, ranks, coils),
+        functools.partial(rows_kernel, blocks, mirror, ranks, coils),
         grid=(per,),
         in_specs=[
-            *(pl.BlockSpec((1, rows, chunk), lambda k, e=e: (e, 0, k)) for e in picks),
-            *(pl.BlockSpec((1, NOTES, chunk), lambda k, e=e: (e, 0, k)) for e in picks),
-        ],
-        out_specs=pl.BlockSpec(shape, lambda k: (0, 0, 0, 0)),
-        out_shape=jax.ShapeDtypeStruct(shape, jnp.bfloat16),
-        scratch_shapes=[pltpu.VMEM((ranks // 2, rows, 2 * LANES), jnp.float32)] if per > 1 else [],
-        compiler_params=pltpu.CompilerParams(vmem_limit_bytes=28 << 20),
+            *(pl.BlockSpec((2, rows, chunk), lambda k: (0, 0, k)) for _ in mids),
+            *(pl.BlockSpec((2, NOTES, chunk), lambda k: (0, 0, k)) for _ in notes),
+            *(once for _ in earlier),
+        ],
+        out_specs=[once] * outs,
+        out_shape=[jax.ShapeDtypeStruct(shape, jnp.bfloat16)] * outs,
+        scratch_shapes=[pltpu.VMEM((ranks // 2, 2, rows, 2 * LANES), jnp.float32)] if per > 1 else [],
+        compiler_params=pltpu.CompilerParams(vmem_limit_bytes=10 << 20),
         cost_estimate=pl.CostEstimate(
-            flops=2 * rows * near * depth * ranks * LANES, bytes_accessed=2 * rows * ranks * LANES, transcendentals=0
+            flops=2 * rows * met * depth * ranks * LANES, bytes_accessed=4 * rows * ranks * LANES, transcendentals=0
         ),
         name="expand_rows",
-    )(*mids, *notes)
-
-
-def image_kernel(count, *refs):
+    )(*mids, *notes, *earlier)
+
+
+def image_kernel(*refs):
     waves_ref, out_ref = refs[-2:]
     plane = out_ref.shape[0]
     half = plane // 2
+    per = (len(refs) - 2) // 2
     groups, pairs, inner, _ = refs[0].shape
-    columns = groups * pairs * inner
-    sums, turns = [], []
-    for direct, mirrored in zip(refs[:count], refs[count : 2 * count]):
-        ahead, behind = direct[...], mirrored[...]
-        sums.append(ahead + behind)
-        gap = (ahead - behind).reshape(groups // 2, 2, pairs, inner, LANES)
-        turns.append(jnp.concatenate([-gap[:, 1:2], gap[:, 0:1]], axis=1).reshape(ahead.shape))
-    lower = lax.broadcasted_iota(jnp.int32, refs[0].shape, 3) < LANES // 2
     halves = []
     for parity in range(2):
-        chosen = [
-            jnp.where(lower, part[n + parity], part[n + 1 - parity]).reshape(columns, LANES)
-            for part in (sums, turns)
-            for n in range(0, count, 2)
-        ]
+        chosen = [ref[...].reshape(groups * pairs * inner, LANES) for ref in refs[parity * per : (parity + 1) * per]]
         halves.append(dot_nt(waves_ref[parity], jnp.concatenate(chosen, axis=1)))
     out_ref[:half, :] = ((halves[0] + halves[1]) * (1.0 / plane)).astype(jnp.bfloat16)
     out_ref[half:, :] = ((halves[0] - halves[1]) * (1.0 / plane)).astype(jnp.bfloat16)
 
 
-def form_image(direct, mirrored, waves):
+def form_image(even, odd, waves):
     plane = 2 * waves.shape[1]
-    groups, pairs, inner, _ = direct[0].shape
+    groups, pairs, inner, _ = even[0].shape
     step = next(n for n in (16, 8, 4, 2) if groups % n == 0)
     columns = step * pairs * inner
     return pl.pallas_call(
-        functools.partial(image_kernel, len(direct)),
+        image_kernel,
         grid=(groups // step,),
         in_specs=[
-            *(pl.BlockSpec((step, pairs, inner, LANES), lambda s: (s, 0, 0, 0)) for _ in (*direct, *mirrored)),
+            *(pl.BlockSpec((step, pairs, inner, LANES), lambda s: (s, 0, 0, 0)) for _ in (*even, *odd)),
             pl.BlockSpec(waves.shape, lambda s: (0, 0, 0)),
         ],
         out_specs=pl.BlockSpec((plane, columns), lambda s: (0, s)),
         out_shape=jax.ShapeDtypeStruct((plane, groups * pairs * inner), jnp.bfloat16),
-        compiler_params=pltpu.CompilerParams(vmem_limit_bytes=24 << 20),
+        compiler_params=pltpu.CompilerParams(vmem_limit_bytes=10 << 20),
         cost_estimate=pl.CostEstimate(
             flops=2 * plane * waves.shape[2] * groups * pairs * inner,
             bytes_accessed=4 * plane * groups * pairs * inner,
             transcendentals=0,
         ),
         name="form_image",
-    )(*direct, *mirrored, waves)
+    )(*even, *odd, waves)
 
 
 def pack_tiles(tiles, tile_rows):
     span = (tile_rows + WIN_ROWS) // 2 + 1
     room = LANES // 2 // span
     blocks = []
+    room = min(room, tiles // 4)
     for first in range(0, tiles // 2, room):
         blocks.append([(t, n * span) for n, t in enumerate(range(first, min(first + room, tiles // 2)))])
-    return blocks + [[]] * (len(blocks) % 2), span
+    return blocks, span
 
 
 def kx_of_lanes(blocks, span):
@@ -464,22 +471,17 @@
         mids.append(mid)
         notes.append(note)
 
-    direct, mirrored = [], []
-    for n, members in enumerate(layout):
-        for mirror, blocks in ((None, direct), (float(tile_rows + WIN_ROWS), mirrored)):
-            met = [(t if mirror is None else t ^ (tiles - 1), seat) for t, seat in members]
-            block = expand_rows(
-                [mids[t // 2] for t, _ in met],
-                [notes[t // 2] for t, _ in met],
-                [t % 2 for t, _ in met],
-                [float(seat) for _, seat in met],
-                n % 2,
-                mirror,
-                ranks,
-                coils,
-            ) if met else jnp.zeros_like(blocks[0])
-            blocks.append(block)
-    return form_image(direct, mirrored, waves)[None]
+    def expand(n, mirror, earlier):
+        met = [[(t if mirror is None else t ^ (tiles - 1), seat) for t, seat in members] for members in layout[n : n + 2]]
+        groups = sorted({t // 2 for members in met for t, _ in members})
+        blocks = [[(groups.index(t // 2), t % 2, float(seat)) for t, seat in members] for members in met]
+        return expand_rows([mids[g] for g in groups], [notes[g] for g in groups], blocks, mirror, earlier, ranks, coils)
+
+    twos = range(0, len(layout), 2)
+    direct = [expand(n, None, ()) for n in twos]
+    folded = [expand(n, float(tile_rows + WIN_ROWS), direct[n // 2]) for n in twos]
+    even, odd_kx = ([part[2 * k + parity] for k in range(2) for part in folded] for parity in range(2))
+    return form_image(even, odd_kx, waves)[None]
 
 
 def solution(mesh):

time: 80.6 us -> 80.2 us (level)
  Pallas kernels: 37.3 us -> 35.7 us
  local copies, waits for them, and re-layouts: 4.53 us -> 5.44 us
    pallas_call x9 -> x5, Pallas kernels: 23.6 us -> 22.1 us  [the longest x1 12.4 us: form_image(): pl.pallas_call(image_kernel, grid=(groups // step,), in_specs=[*(pl.Block...]
    ppermute x7, waiting for transfers between devices: 16.6 us -> 17.9 us  [from_tiles(): lax.ppermute(value, 'tile', [(source_of(t), t) for t in range(count)])]
    unnamed x13, local copies, waits for them, and re-layouts: 2.37 us -> 3.28 us
    all_to_all x1, waiting for transfers between devices: 4.49 us -> 3.65 us  [body(): lax.all_to_all(packed, ('kz', 'tile'), split_axis=0, concat_axis=0, tiled...]
  transfers between devices with their start and end apart: 8 -> 8, of which waited for: 5 -> 5; matrix products, arithmetic and copies ran while one was open for 7% -> 7% of each run, Pallas kernels for 15% -> 16%
where the time goes in v2:
time: 80.2 us; the launch traced here: 79.7 us
  Pallas kernels  35.7 us (45%)
  waiting for transfers between devices  21.6 us (27%)
  starting transfers between devices  13.9 us (17%)
  local copies, waits for them, and re-layouts  5.44 us (7%)
  other arithmetic  2.79 us (3%)
    ppermute x7, waiting for transfers between devices, from_tiles(): lax.ppermute(value, 'tile', [(source_of(t), t) for t in range(count)])  17.9 us
    pallas_call x1, Pallas kernels, form_image(): pl.pallas_call(image_kernel, grid=(groups // step,), in_specs=[*(pl.Block...  12.4 us
    pallas_call x4, Pallas kernels, expand_rows(): pl.pallas_call(functools.partial(rows_kernel, blocks, mirror, ranks, coil...  9.68 us
    all_to_all x1, starting transfers between devices, body(): lax.all_to_all(packed, ('kz', 'tile'), split_axis=0, concat_axis=0, tiled...  7.44 us
    pallas_call x4, Pallas kernels, transform_columns(): pl.pallas_call(functools.partial(columns_kernel, coils), grid=(2, per), i...  6.6 us
    ppermute x7, starting transfers between devices, from_tiles(): lax.ppermute(value, 'tile', [(source_of(t), t) for t in range(count)])  6.46 us
    pallas_call x1, Pallas kernels, grid_windows(): pl.pallas_call(functools.partial(window_kernel, slots, pair), grid=(devic...  3.94 us
    all_to_all x1, waiting for transfers between devices, body(): lax.all_to_all(packed, ('kz', 'tile'), split_axis=0, concat_axis=0, tiled...  3.65 us
  transfers between devices with their start and end apart: 8, of which 5 were waited for; matrix products, arithmetic and copies ran while one was open for 7% of the time, Pallas kernels for 16%

profile of v2, /device:TPU:0, one launch (start us, length us, event | category | flops | bytes accessed | tf_op | source)
XLA Modules:
  0.0 79.7 jit_solution(17045926224757948214)
XLA Ops:
  0.0 2.2 %pack_slots.1 = bf16[32,40,128]{2,1,0:T(8,128)(2,1)} custom-call(s32[1,1,4,2,8]{4,3,2,1,0:T(2,128)} %bitcast.21, bf16[1,1,4,8,2,16,128]{6,5,4,3,2,1,0:T(8,128)(2,1)} %data_ref.1, bf16[10,1000]{1,0:T(8,128)(2,1)} %bitcast.20), custom_call_target="tpu_custom_call" | custom-call | tf_op jit(solution)/shard_map/pack_slots/pallas_call | solution.py:112
  2.2 7.4 %all-to-all-start = ((bf16[32,40,128]{2,1,0:T(8,128)(2,1)}), bf16[32,40,128]{2,1,0:T(8,128)(2,1)}, u32[]{:S(2)}, u32[]{:S(2)}) async-start(bf16[32,40,128]{2,1,0:T(8,128)(2,1)} %pack_slots.1), calls=%async_computation | async-start | bytes 655360 | tf_op jit(solution)/shard_map/all_to_all | solution.py:431
  11.8 1.0 %bitcast_select_fusion = f32[64,2,128]{2,1,0:T(2,128)S(1)} fusion(f32[1,1,4,8,2,2,128]{6,5,4,3,2,1,0:T(2,128)} %param.12, pred[64]{0:T(512)(128)(4,1)S(1)} %lt.60), kind=kLoop, calls=%fused_computation.3 | loop fusion | flops 16384 | bytes 131136 | tf_op jit(solution)/shard_map/jit(_where)/select_n | solution.py:436
  12.9 1.0 %constant_dynamic-slice_fusion.rows_ref.wave_ref = bf16[80,1280]{1,0:T(8,128)(2,1)S(1)} fusion(bf16[640,1280]{1,0:T(8,128)(2,1)} %constant.112.clone.wave_ref, s32[]{:T(128)S(6)} %select_n.70), kind=kLoop, calls=%fused_computation.16 | loop fusion | bytes 409604 | tf_op jit(solution)/shard_map/dynamic_slice | solution.py:450
  14.6 0.9 %make_tables.1 = (bf16[1280,512]{1,0:T(8,128)(2,1)S(1)}, bf16[2,320,512]{2,1,0:T(8,128)(2,1)S(1)}) custom-call(bf16[640,1280]{1,0:T(8,128)(2,1)S(1)} %copy-done.3, bf16[80,1280]{1,0:T(8,128)(2,1)S(1)} %constant_dynamic-slice_fusion.rows_ref.wave_ref, s32[2,256]{1,0:T(2,128)S(1)} %fusion.lanes_ref), custom_call_target="tpu_custom_call" | custom-call | tf_op jit(solution)/shard_map/make_tables/pallas_call | solution.py:78
  16.3 0.8 %copy-done.4 = bf16[2,320,512]{2,1,0:T(8,128)(2,1)} copy-done((bf16[2,320,512]{2,1,0:T(8,128)(2,1)}, bf16[2,320,512]{2,1,0:T(8,128)(2,1)S(1)}, u32[]{:S(2)}) %copy-start.4) | copy-done | bytes 655384
  18.0 3.7 %all-to-all-done.data_ref.rate_ref = bf16[32,40,128]{2,1,0:T(8,128)(2,1)} async-done(((bf16[32,40,128]{2,1,0:T(8,128)(2,1)}), bf16[32,40,128]{2,1,0:T(8,128)(2,1)}, u32[]{:S(2)}, u32[]{:S(2)}) %all-to-all-start) | async-done | bytes 327712 | tf_op jit(solution)/shard_map/all_to_all | solution.py:431
  21.7 3.9 %grid_windows.1.mine_ref.mine_notes = bf16[272,512]{1,0:T(8,128)(2,1)} custom-call(bf16[32,40,128]{2,1,0:T(8,128)(2,1)} %all-to-all-done.data_ref.rate_ref, bf16[32,40,128]{2,1,0:T(8,128)(2,1)} %all-to-all-done.data_ref.rate_ref, bf16[64,128,128]{2,1,0:T(8,128)(2,1)S(1)} %bitcast.17, f32[16,256]{1,0:T(8,128)S(1)} %pad.4.place_ref), custom_call_target="tpu_custom_call" | custom-call | tf_op jit(solution)/shard_map/grid_windows/pallas_call | solution.py:172
  25.6 1.6 %collective-permute-start.5 = (bf16[272,512]{1,0:T(8,128)(2,1)}, bf16[272,512]{1,0:T(8,128)(2,1)S(1)}, u32[]{:S(2)}, u32[]{:S(2)}) collective-permute-start(bf16[272,512]{1,0:T(8,128)(2,1)} %grid_windows.1.mine_ref.mine_notes), channel_id=1, source_target_pairs={{2,0},{3,1},{0,2},{1,3},{6,4},{7,5},{4,6},{5,7},{10,8},{11,9},{8,1... | collective-permute-start | bytes 835592 | tf_op jit(solution)/shard_map/ppermute | solution.py:411
  27.3 1.4 %collective-permute-start.3 = (bf16[272,512]{1,0:T(8,128)(2,1)}, bf16[272,512]{1,0:T(8,128)(2,1)S(1)}, u32[]{:S(2)}, u32[]{:S(2)}) collective-permute-start(bf16[272,512]{1,0:T(8,128)(2,1)} %grid_windows.1.mine_ref.mine_notes), channel_id=1, source_target_pairs={{1,0},{0,1},{3,2},{2,3},{5,4},{4,5},{7,6},{6,7},{9,8},{8,9},{11,10... | collective-permute-start | bytes 835592 | tf_op jit(solution)/shard_map/ppermute | solution.py:411
  28.6 12.4 %collective-permute-done.mine_ref.mine_notes = bf16[272,512]{1,0:T(8,128)(2,1)S(1)} collective-permute-done((bf16[272,512]{1,0:T(8,128)(2,1)}, bf16[272,512]{1,0:T(8,128)(2,1)S(1)}, u32[]{:S(2)}, u32[]{:S(2)}) %collective-permute-start) | collective-permute-done | bytes 278560 | tf_op jit(solution)/shard_map/ppermute | solution.py:411
  41.7 1.3 %collective-permute-start.4 = (bf16[272,512]{1,0:T(8,128)(2,1)S(1)}, bf16[272,512]{1,0:T(8,128)(2,1)S(1)}, u32[]{:S(2)}, u32[]{:S(2)}) collective-permute-start(bf16[272,512]{1,0:T(8,128)(2,1)S(1)} %collective-permute-done.mine_ref.mine_notes), channel_id=1, source_target_pairs={{1,0},{0,1},{3,2},{2,3},{5,4},{4,5},{7,6},{6,7},{9,8},{8,9},{11,10... | collective-permute-start | bytes 835592 | tf_op jit(solution)/shard_map/ppermute | solution.py:411
  43.1 0.9 %copy-done.1 = bf16[80,1280]{1,0:T(8,128)(2,1)S(1)} copy-done((bf16[80,1280]{1,0:T(8,128)(2,1)S(1)}, bf16[80,1280]{1,0:T(8,128)(2,1)}, u32[]{:S(2)}) %copy-start.1) | copy-done | bytes 204824
  44.0 2.3 %transform_columns.5 = (bf16[2,1280,256]{2,1,0:T(8,128)(2,1)S(1)}, bf16[2,16,256]{2,1,0:T(8,128)(2,1)S(1)}) custom-call(s32[1]{0:T(128)} %bitcast.odd_ref, bf16[272,512]{1,0:T(8,128)(2,1)} %grid_windows.1.mine_ref.mine_notes, bf16[272,512]{1,0:T(8,128)(2,1)} %grid_windows.1.mine_ref.mine_notes, ...), custom_call_target="tpu_custom_call" | custom-call | flops 671088640 | bytes 1310720 | tf_op jit(solution)/shard_map/transform_columns/pallas_call | solution.py:225
  46.3 1.9 %expand_rows.4 = (bf16[160,5,16,128]{3,2,1,0:T(8,128)(2,1)S(1)}, bf16[160,5,16,128]{3,2,1,0:T(8,128)(2,1)S(1)}) custom-call(bf16[2,1280,256]{2,1,0:T(8,128)(2,1)S(1)} %get-tuple-element.40.refs_0_, bf16[2,16,256]{2,1,0:T(8,128)(2,1)S(1)} %get-tuple-element.41.refs_1_), custom_call_target="tpu_custom_call" | custom-call | flops 1677721600 | bytes 6553600 | tf_op jit(solution)/shard_map/expand_rows/pallas_call | solution.py:330
  48.9 1.4 %collective-permute-start.2 = (bf16[272,512]{1,0:T(8,128)(2,1)S(1)}, bf16[272,512]{1,0:T(8,128)(2,1)S(1)}, u32[]{:S(2)}, u32[]{:S(2)}) collective-permute-start(bf16[272,512]{1,0:T(8,128)(2,1)S(1)} %collective-permute-done.1.mine_ref.mine_notes), channel_id=1, source_target_pairs={{1,0},{0,1},{3,2},{2,3},{5,4},{4,5},{7,6},{6,7},{9,8},{8,9},{11,10... | collective-permute-start | bytes 835592 | tf_op jit(solution)/shard_map/ppermute | solution.py:411
  50.6 1.4 %transform_columns.7 = (bf16[2,1280,256]{2,1,0:T(8,128)(2,1)S(1)}, bf16[2,16,256]{2,1,0:T(8,128)(2,1)S(1)}) custom-call(s32[1]{0:T(128)} %bitcast.odd_ref, bf16[272,512]{1,0:T(8,128)(2,1)S(1)} %collective-permute-done.5.mine_ref.mine_notes, bf16[272,512]{1,0:T(8,128)(2,1)S(1)} %collective-permute-done.5.mine_ref.mine_notes, ...), custom_call_target="tpu_custom_call" | custom-call | flops 671088640 | bytes 1310720 | tf_op jit(solution)/shard_map/transform_columns/pallas_call | solution.py:225
  51.9 4.6 %collective-permute-done.4.other_ref.other_notes = bf16[272,512]{1,0:T(8,128)(2,1)S(1)} collective-permute-done((bf16[272,512]{1,0:T(8,128)(2,1)S(1)}, bf16[272,512]{1,0:T(8,128)(2,1)S(1)}, u32[]{:S(2)}, u32[]{:S(2)}) %collective-permute-start.4) | collective-permute-done | bytes 278560 | tf_op jit(solution)/shard_map/ppermute | solution.py:411
  56.5 1.4 %transform_columns.6 = (bf16[2,1280,256]{2,1,0:T(8,128)(2,1)S(1)}, bf16[2,16,256]{2,1,0:T(8,128)(2,1)S(1)}) custom-call(s32[1]{0:T(128)} %bitcast.odd_ref, bf16[272,512]{1,0:T(8,128)(2,1)S(1)} %collective-permute-done.mine_ref.mine_notes, bf16[272,512]{1,0:T(8,128)(2,1)S(1)} %collective-permute-done.mine_ref.mine_notes, ...), custom_call_target="tpu_custom_call" | custom-call | flops 671088640 | bytes 1310720 | tf_op jit(solution)/shard_map/transform_columns/pallas_call | solution.py:225
  57.9 1.9 %expand_rows.6 = (bf16[160,5,16,128]{3,2,1,0:T(8,128)(2,1)S(1)}, bf16[160,5,16,128]{3,2,1,0:T(8,128)(2,1)S(1)}) custom-call(bf16[2,1280,256]{2,1,0:T(8,128)(2,1)S(1)} %get-tuple-element.47.refs_0_, bf16[2,16,256]{2,1,0:T(8,128)(2,1)S(1)} %get-tuple-element.48.refs_1_), custom_call_target="tpu_custom_call" | custom-call | flops 1677721600 | bytes 6553600 | tf_op jit(solution)/shard_map/expand_rows/pallas_call | solution.py:330
  59.8 3.0 %expand_rows.7 = (bf16[160,5,16,128]{3,2,1,0:T(8,128)(2,1)S(1)}, bf16[160,5,16,128]{3,2,1,0:T(8,128)(2,1)S(1)}, bf16[160,5,16,128]{3,2,1,0:T(8,128)(2,1)S(1)}, bf16[160,5,16,128]{3,2,1,0:T(8,128)(2,1)S(1)}) custom-call(bf16[2,1280,256]{2,1,0:T(8,128)(2,1)S(1)} %get-tuple-element.45.refs_0_, bf16[2,16,256]{2,1,0:T(8,128)(2,1)S(1)} %get-tuple-element.46.refs_1_, ...), custom_call_target="tpu_custom_call" | custom-call | flops 1677721600 | bytes 6553600 | tf_op jit(solution)/shard_map/expand_rows/pallas_call | solution.py:330
  62.8 1.6 %transform_columns.4 = (bf16[2,1280,256]{2,1,0:T(8,128)(2,1)S(1)}, bf16[2,16,256]{2,1,0:T(8,128)(2,1)S(1)}) custom-call(s32[1]{0:T(128)} %bitcast.odd_ref, bf16[272,512]{1,0:T(8,128)(2,1)S(1)} %collective-permute-done.1.mine_ref.mine_notes, bf16[272,512]{1,0:T(8,128)(2,1)S(1)} %collective-permute-done.1.mine_ref.mine_notes, ...), custom_call_target="tpu_custom_call" | custom-call | flops 671088640 | bytes 1310720 | tf_op jit(solution)/shard_map/transform_columns/pallas_call | solution.py:225
  64.4 2.9 %expand_rows.5 = (bf16[160,5,16,128]{3,2,1,0:T(8,128)(2,1)S(1)}, bf16[160,5,16,128]{3,2,1,0:T(8,128)(2,1)S(1)}, bf16[160,5,16,128]{3,2,1,0:T(8,128)(2,1)S(1)}, bf16[160,5,16,128]{3,2,1,0:T(8,128)(2,1)S(1)}) custom-call(bf16[2,1280,256]{2,1,0:T(8,128)(2,1)S(1)} %get-tuple-element.38.refs_0_, bf16[2,16,256]{2,1,0:T(8,128)(2,1)S(1)} %get-tuple-element.39.refs_1_, ...), custom_call_target="tpu_custom_call" | custom-call | flops 1677721600 | bytes 6553600 | tf_op jit(solution)/shard_map/expand_rows/pallas_call | solution.py:330
  67.3 12.4 %form_image.1 = bf16[640,12800]{1,0:T(8,128)(2,1)} custom-call(bf16[160,5,16,128]{3,2,1,0:T(8,128)(2,1)S(1)} %get-tuple-element.44.refs_0_, bf16[160,5,16,128]{3,2,1,0:T(8,128)(2,1)S(1)} %get-tuple-element.51.refs_1_, bf16[160,5,16,128]{3,2,1,0:T(8,128)(2,1)S(1)} %get-tuple-element.52.refs_2_, bf16[160,5,16,128]{3,2,1,0:T(8,128)(2,1)S(1)} %get-tuple-element.53.refs_3_, ...), custom_call_target="tpu_custom_call" | custom-call | flops 8388608000 | bytes 32768000 | tf_op jit(solution)/shard_map/form_image/pallas_call | solution.py:368
  (37 shorter events, 6.2 us)
Async XLA Ops:
  0.0 14.6 %copy-start.3 = (bf16[640,1280]{1,0:T(8,128)(2,1)S(1)}, bf16[640,1280]{1,0:T(8,128)(2,1)}, u32[]{:S(2)}) copy-start(bf16[640,1280]{1,0:T(8,128)(2,1)} %constant.112.clone.wave_ref) | copy-start | bytes 4915204
  2.2 19.5 %all-to-all-start = ((bf16[32,40,128]{2,1,0:T(8,128)(2,1)}), bf16[32,40,128]{2,1,0:T(8,128)(2,1)}, u32[]{:S(2)}, u32[]{:S(2)}) async-start(bf16[32,40,128]{2,1,0:T(8,128)(2,1)} %pack_slots.1), calls=%async_computation | async-start | bytes 655360 | tf_op jit(solution)/shard_map/all_to_all | solution.py:431
  15.6 0.7 copy-start
  16.3 0.8 %copy-start.4 = (bf16[2,320,512]{2,1,0:T(8,128)(2,1)}, bf16[2,320,512]{2,1,0:T(8,128)(2,1)S(1)}, u32[]{:S(2)}) copy-start(bf16[2,320,512]{2,1,0:T(8,128)(2,1)S(1)} %get-tuple-element.58.refs_8_) | copy-start | bytes 1966084
  25.6 15.4 %collective-permute-start = (bf16[272,512]{1,0:T(8,128)(2,1)}, bf16[272,512]{1,0:T(8,128)(2,1)S(1)}, u32[]{:S(2)}, u32[]{:S(2)}) collective-permute-start(bf16[272,512]{1,0:T(8,128)(2,1)} %grid_windows.1.mine_ref.mine_notes), channel_id=1, source_target_pairs={{4,0},{5,1},{6,2},{7,3},{0,4},{1,5},{2,6},{3,7},{12,8},{13,9},{14,... | collective-permute-start | bytes 835592 | tf_op jit(solution)/shard_map/ppermute | solution.py:411
  25.6 15.4 %collective-permute-start.5 = (bf16[272,512]{1,0:T(8,128)(2,1)}, bf16[272,512]{1,0:T(8,128)(2,1)S(1)}, u32[]{:S(2)}, u32[]{:S(2)}) collective-permute-start(bf16[272,512]{1,0:T(8,128)(2,1)} %grid_windows.1.mine_ref.mine_notes), channel_id=1, source_target_pairs={{2,0},{3,1},{0,2},{1,3},{6,4},{7,5},{4,6},{5,7},{10,8},{11,9},{8,1... | collective-permute-start | bytes 835592 | tf_op jit(solution)/shard_map/ppermute | solution.py:411
  27.3 15.8 %collective-permute-start.3 = (bf16[272,512]{1,0:T(8,128)(2,1)}, bf16[272,512]{1,0:T(8,128)(2,1)S(1)}, u32[]{:S(2)}, u32[]{:S(2)}) collective-permute-start(bf16[272,512]{1,0:T(8,128)(2,1)} %grid_windows.1.mine_ref.mine_notes), channel_id=1, source_target_pairs={{1,0},{0,1},{3,2},{2,3},{5,4},{4,5},{7,6},{6,7},{9,8},{8,9},{11,10... | collective-permute-start | bytes 835592 | tf_op jit(solution)/shard_map/ppermute | solution.py:411
  41.0 7.9 %collective-permute-start.1 = (bf16[272,512]{1,0:T(8,128)(2,1)S(1)}, bf16[272,512]{1,0:T(8,128)(2,1)S(1)}, u32[]{:S(2)}, u32[]{:S(2)}) collective-permute-start(bf16[272,512]{1,0:T(8,128)(2,1)S(1)} %collective-permute-done.mine_ref.mine_notes), channel_id=1, source_target_pairs={{2,0},{3,1},{0,2},{1,3},{6,4},{7,5},{4,6},{5,7},{10,8},{11,9},{8,1... | collective-permute-start | bytes 835592 | tf_op jit(solution)/shard_map/ppermute | solution.py:411
  41.0 9.5 %collective-permute-start.6 = (bf16[272,512]{1,0:T(8,128)(2,1)S(1)}, bf16[272,512]{1,0:T(8,128)(2,1)S(1)}, u32[]{:S(2)}, u32[]{:S(2)}) collective-permute-start(bf16[272,512]{1,0:T(8,128)(2,1)S(1)} %collective-permute-done.5.mine_ref.mine_notes), channel_id=1, source_target_pairs={{1,0},{0,1},{3,2},{2,3},{5,4},{4,5},{7,6},{6,7},{9,8},{8,9},{11,10... | collective-permute-start | bytes 835592 | tf_op jit(solution)/shard_map/ppermute | solution.py:411
  41.7 14.8 %collective-permute-start.4 = (bf16[272,512]{1,0:T(8,128)(2,1)S(1)}, bf16[272,512]{1,0:T(8,128)(2,1)S(1)}, u32[]{:S(2)}, u32[]{:S(2)}) collective-permute-start(bf16[272,512]{1,0:T(8,128)(2,1)S(1)} %collective-permute-done.mine_ref.mine_notes), channel_id=1, source_target_pairs={{1,0},{0,1},{3,2},{2,3},{5,4},{4,5},{7,6},{6,7},{9,8},{8,9},{11,10... | collective-permute-start | bytes 835592 | tf_op jit(solution)/shard_map/ppermute | solution.py:411
  43.1 0.9 %copy-start.1 = (bf16[80,1280]{1,0:T(8,128)(2,1)S(1)}, bf16[80,1280]{1,0:T(8,128)(2,1)}, u32[]{:S(2)}) copy-start(bf16[80,1280]{1,0:T(8,128)(2,1)} %copy-done) | copy-start | bytes 614404
  46.3 4.3 %copy-start.2 = (bf16[80,1280]{1,0:T(8,128)(2,1)S(1)}, bf16[80,1280]{1,0:T(8,128)(2,1)}, u32[]{:S(2)}) copy-start(bf16[80,1280]{1,0:T(8,128)(2,1)} %copy-done) | copy-start | bytes 614404
  48.9 13.9 %collective-permute-start.2 = (bf16[272,512]{1,0:T(8,128)(2,1)S(1)}, bf16[272,512]{1,0:T(8,128)(2,1)S(1)}, u32[]{:S(2)}, u32[]{:S(2)}) collective-permute-start(bf16[272,512]{1,0:T(8,128)(2,1)S(1)} %collective-permute-done.1.mine_ref.mine_notes), channel_id=1, source_target_pairs={{1,0},{0,1},{3,2},{2,3},{5,4},{4,5},{7,6},{6,7},{9,8},{8,9},{11,10... | collective-permute-start | bytes 835592 | tf_op jit(solution)/shard_map/ppermute | solution.py:411
  64.4 2.9 %copy-start.5 = (bf16[2,320,512]{2,1,0:T(8,128)(2,1)S(1)}, bf16[2,320,512]{2,1,0:T(8,128)(2,1)}, u32[]{:S(2)}) copy-start(bf16[2,320,512]{2,1,0:T(8,128)(2,1)} %copy-done.4) | copy-start | bytes 1966084

commit v3 on v2

--- a/solution.py
+++ b/solution.py
@@ -166,7 +166,7 @@
     count = devices * slots
     depth = count * WIN_ROWS
     width = WIN_COLS * pair
-    sources = 8
+    sources = 16
     rate_rows = slots * WIN_ROWS
     total_rows = depth + NOTES * (depth // min(depth, width))
     return pl.pallas_call(
@@ -363,7 +363,7 @@
 def form_image(even, odd, waves):
     plane = 2 * waves.shape[1]
     groups, pairs, inner, _ = even[0].shape
-    step = next(n for n in (16, 8, 4, 2) if groups % n == 0)
+    step = next(n for n in (32, 16, 8, 4, 2) if groups % n == 0)
     columns = step * pairs * inner
     return pl.pallas_call(
         image_kernel,
@@ -374,7 +374,7 @@
         ],
         out_specs=pl.BlockSpec((plane, columns), lambda s: (0, s)),
         out_shape=jax.ShapeDtypeStruct((plane, groups * pairs * inner), jnp.bfloat16),
-        compiler_params=pltpu.CompilerParams(vmem_limit_bytes=10 << 20),
+        compiler_params=pltpu.CompilerParams(vmem_limit_bytes=20 << 20),
         cost_estimate=pl.CostEstimate(
             flops=2 * plane * waves.shape[2] * groups * pairs * inner,
             bytes_accessed=4 * plane * groups * pairs * inner,

time: 80.2 us -> 78.6 us (0.980)
  Pallas kernels: 35.7 us -> 34.3 us
    pallas_call x1, Pallas kernels: 12.4 us -> 11.5 us  [form_image(): pl.pallas_call(image_kernel, grid=(groups // step,), in_specs=[*(pl.Block...]
where the time goes in v3:
time: 78.6 us; the launch traced here: 78.2 us
  Pallas kernels  34.3 us (44%)
  waiting for transfers between devices  21.6 us (27%)
  starting transfers between devices  13.9 us (18%)
  local copies, waits for them, and re-layouts  5.44 us (7%)
  other arithmetic  2.79 us (4%)
    ppermute x7, waiting for transfers between devices, from_tiles(): lax.ppermute(value, 'tile', [(source_of(t), t) for t in range(count)])  17.9 us
    pallas_call x1, Pallas kernels, form_image(): pl.pallas_call(image_kernel, grid=(groups // step,), in_specs=[*(pl.Block...  11.5 us
    pallas_call x4, Pallas kernels, expand_rows(): pl.pallas_call(functools.partial(rows_kernel, blocks, mirror, ranks, coil...  9.68 us
    all_to_all x1, starting transfers between devices, body(): lax.all_to_all(packed, ('kz', 'tile'), split_axis=0, concat_axis=0, tiled...  7.44 us
    pallas_call x4, Pallas kernels, transform_columns(): pl.pallas_call(functools.partial(columns_kernel, coils), grid=(2, per), i...  6.63 us
    ppermute x7, starting transfers between devices, from_tiles(): lax.ppermute(value, 'tile', [(source_of(t), t) for t in range(count)])  6.46 us
    all_to_all x1, waiting for transfers between devices, body(): lax.all_to_all(packed, ('kz', 'tile'), split_axis=0, concat_axis=0, tiled...  3.65 us
    pallas_call x1, Pallas kernels, grid_windows(): pl.pallas_call(functools.partial(window_kernel, slots, pair), grid=(devic...  3.29 us
  transfers between devices with their start and end apart: 8, of which 5 were waited for; matrix products, arithmetic and copies ran while one was open for 7% of the time, Pallas kernels for 16%

profile of v3, /device:TPU:0, one launch (start us, length us, event | category | flops | bytes accessed | tf_op | source)
XLA Modules:
  0.0 78.2 jit_solution(8179131454829703108)
XLA Ops:
  0.0 2.2 %pack_slots.1 = bf16[32,40,128]{2,1,0:T(8,128)(2,1)} custom-call(s32[1,1,4,2,8]{4,3,2,1,0:T(2,128)} %bitcast.21, bf16[1,1,4,8,2,16,128]{6,5,4,3,2,1,0:T(8,128)(2,1)} %data_ref.1, bf16[10,1000]{1,0:T(8,128)(2,1)} %bitcast.20), custom_call_target="tpu_custom_call" | custom-call | tf_op jit(solution)/shard_map/pack_slots/pallas_call | solution.py:112
  2.2 7.4 %all-to-all-start = ((bf16[32,40,128]{2,1,0:T(8,128)(2,1)}), bf16[32,40,128]{2,1,0:T(8,128)(2,1)}, u32[]{:S(2)}, u32[]{:S(2)}) async-start(bf16[32,40,128]{2,1,0:T(8,128)(2,1)} %pack_slots.1), calls=%async_computation | async-start | bytes 655360 | tf_op jit(solution)/shard_map/all_to_all | solution.py:431
  11.8 1.0 %bitcast_select_fusion = f32[64,2,128]{2,1,0:T(2,128)S(1)} fusion(f32[1,1,4,8,2,2,128]{6,5,4,3,2,1,0:T(2,128)} %param.12, pred[64]{0:T(512)(128)(4,1)S(1)} %lt.60), kind=kLoop, calls=%fused_computation.3 | loop fusion | flops 16384 | bytes 131136 | tf_op jit(solution)/shard_map/jit(_where)/select_n | solution.py:436
  12.9 1.0 %constant_dynamic-slice_fusion.rows_ref.wave_ref = bf16[80,1280]{1,0:T(8,128)(2,1)S(1)} fusion(bf16[640,1280]{1,0:T(8,128)(2,1)} %constant.112.clone.wave_ref, s32[]{:T(128)S(6)} %select_n.70), kind=kLoop, calls=%fused_computation.16 | loop fusion | bytes 409604 | tf_op jit(solution)/shard_map/dynamic_slice | solution.py:450
  14.6 0.9 %make_tables.1 = (bf16[1280,512]{1,0:T(8,128)(2,1)S(1)}, bf16[2,320,512]{2,1,0:T(8,128)(2,1)S(1)}) custom-call(bf16[640,1280]{1,0:T(8,128)(2,1)S(1)} %copy-done.3, bf16[80,1280]{1,0:T(8,128)(2,1)S(1)} %constant_dynamic-slice_fusion.rows_ref.wave_ref, s32[2,256]{1,0:T(2,128)S(1)} %fusion.lanes_ref), custom_call_target="tpu_custom_call" | custom-call | tf_op jit(solution)/shard_map/make_tables/pallas_call | solution.py:78
  16.3 0.8 %copy-done.4 = bf16[2,320,512]{2,1,0:T(8,128)(2,1)} copy-done((bf16[2,320,512]{2,1,0:T(8,128)(2,1)}, bf16[2,320,512]{2,1,0:T(8,128)(2,1)S(1)}, u32[]{:S(2)}) %copy-start.4) | copy-done | bytes 655384
  18.0 3.7 %all-to-all-done.data_ref.rate_ref = bf16[32,40,128]{2,1,0:T(8,128)(2,1)} async-done(((bf16[32,40,128]{2,1,0:T(8,128)(2,1)}), bf16[32,40,128]{2,1,0:T(8,128)(2,1)}, u32[]{:S(2)}, u32[]{:S(2)}) %all-to-all-start) | async-done | bytes 327712 | tf_op jit(solution)/shard_map/all_to_all | solution.py:431
  21.7 3.3 %grid_windows.1.mine_ref.mine_notes = bf16[272,512]{1,0:T(8,128)(2,1)} custom-call(bf16[32,40,128]{2,1,0:T(8,128)(2,1)} %all-to-all-done.data_ref.rate_ref, bf16[32,40,128]{2,1,0:T(8,128)(2,1)} %all-to-all-done.data_ref.rate_ref, bf16[64,128,128]{2,1,0:T(8,128)(2,1)S(1)} %bitcast.17, f32[16,256]{1,0:T(8,128)S(1)} %pad.4.place_ref), custom_call_target="tpu_custom_call" | custom-call | tf_op jit(solution)/shard_map/grid_windows/pallas_call | solution.py:172
  25.0 1.6 %collective-permute-start.5 = (bf16[272,512]{1,0:T(8,128)(2,1)}, bf16[272,512]{1,0:T(8,128)(2,1)S(1)}, u32[]{:S(2)}, u32[]{:S(2)}) collective-permute-start(bf16[272,512]{1,0:T(8,128)(2,1)} %grid_windows.1.mine_ref.mine_notes), channel_id=1, source_target_pairs={{2,0},{3,1},{0,2},{1,3},{6,4},{7,5},{4,6},{5,7},{10,8},{11,9},{8,1... | collective-permute-start | bytes 835592 | tf_op jit(solution)/shard_map/ppermute | solution.py:411
  26.6 1.4 %collective-permute-start.3 = (bf16[272,512]{1,0:T(8,128)(2,1)}, bf16[272,512]{1,0:T(8,128)(2,1)S(1)}, u32[]{:S(2)}, u32[]{:S(2)}) collective-permute-start(bf16[272,512]{1,0:T(8,128)(2,1)} %grid_windows.1.mine_ref.mine_notes), channel_id=1, source_target_pairs={{1,0},{0,1},{3,2},{2,3},{5,4},{4,5},{7,6},{6,7},{9,8},{8,9},{11,10... | collective-permute-start | bytes 835592 | tf_op jit(solution)/shard_map/ppermute | solution.py:411
  28.0 12.4 %collective-permute-done.mine_ref.mine_notes = bf16[272,512]{1,0:T(8,128)(2,1)S(1)} collective-permute-done((bf16[272,512]{1,0:T(8,128)(2,1)}, bf16[272,512]{1,0:T(8,128)(2,1)S(1)}, u32[]{:S(2)}, u32[]{:S(2)}) %collective-permute-start) | collective-permute-done | bytes 278560 | tf_op jit(solution)/shard_map/ppermute | solution.py:411
  41.1 1.3 %collective-permute-start.4 = (bf16[272,512]{1,0:T(8,128)(2,1)S(1)}, bf16[272,512]{1,0:T(8,128)(2,1)S(1)}, u32[]{:S(2)}, u32[]{:S(2)}) collective-permute-start(bf16[272,512]{1,0:T(8,128)(2,1)S(1)} %collective-permute-done.mine_ref.mine_notes), channel_id=1, source_target_pairs={{1,0},{0,1},{3,2},{2,3},{5,4},{4,5},{7,6},{6,7},{9,8},{8,9},{11,10... | collective-permute-start | bytes 835592 | tf_op jit(solution)/shard_map/ppermute | solution.py:411
  42.4 0.9 %copy-done.1 = bf16[80,1280]{1,0:T(8,128)(2,1)S(1)} copy-done((bf16[80,1280]{1,0:T(8,128)(2,1)S(1)}, bf16[80,1280]{1,0:T(8,128)(2,1)}, u32[]{:S(2)}) %copy-start.1) | copy-done | bytes 204824
  43.3 2.3 %transform_columns.5 = (bf16[2,1280,256]{2,1,0:T(8,128)(2,1)S(1)}, bf16[2,16,256]{2,1,0:T(8,128)(2,1)S(1)}) custom-call(s32[1]{0:T(128)} %bitcast.odd_ref, bf16[272,512]{1,0:T(8,128)(2,1)} %grid_windows.1.mine_ref.mine_notes, bf16[272,512]{1,0:T(8,128)(2,1)} %grid_windows.1.mine_ref.mine_notes, ...), custom_call_target="tpu_custom_call" | custom-call | flops 671088640 | bytes 1310720 | tf_op jit(solution)/shard_map/transform_columns/pallas_call | solution.py:225
  45.7 1.9 %expand_rows.4 = (bf16[160,5,16,128]{3,2,1,0:T(8,128)(2,1)S(1)}, bf16[160,5,16,128]{3,2,1,0:T(8,128)(2,1)S(1)}) custom-call(bf16[2,1280,256]{2,1,0:T(8,128)(2,1)S(1)} %get-tuple-element.40.refs_0_, bf16[2,16,256]{2,1,0:T(8,128)(2,1)S(1)} %get-tuple-element.41.refs_1_), custom_call_target="tpu_custom_call" | custom-call | flops 1677721600 | bytes 6553600 | tf_op jit(solution)/shard_map/expand_rows/pallas_call | solution.py:330
  48.2 1.4 %collective-permute-start.2 = (bf16[272,512]{1,0:T(8,128)(2,1)S(1)}, bf16[272,512]{1,0:T(8,128)(2,1)S(1)}, u32[]{:S(2)}, u32[]{:S(2)}) collective-permute-start(bf16[272,512]{1,0:T(8,128)(2,1)S(1)} %collective-permute-done.1.mine_ref.mine_notes), channel_id=1, source_target_pairs={{1,0},{0,1},{3,2},{2,3},{5,4},{4,5},{7,6},{6,7},{9,8},{8,9},{11,10... | collective-permute-start | bytes 835592 | tf_op jit(solution)/shard_map/ppermute | solution.py:411
  49.9 1.4 %transform_columns.7 = (bf16[2,1280,256]{2,1,0:T(8,128)(2,1)S(1)}, bf16[2,16,256]{2,1,0:T(8,128)(2,1)S(1)}) custom-call(s32[1]{0:T(128)} %bitcast.odd_ref, bf16[272,512]{1,0:T(8,128)(2,1)S(1)} %collective-permute-done.5.mine_ref.mine_notes, bf16[272,512]{1,0:T(8,128)(2,1)S(1)} %collective-permute-done.5.mine_ref.mine_notes, ...), custom_call_target="tpu_custom_call" | custom-call | flops 671088640 | bytes 1310720 | tf_op jit(solution)/shard_map/transform_columns/pallas_call | solution.py:225
  51.3 4.6 %collective-permute-done.4.other_ref.other_notes = bf16[272,512]{1,0:T(8,128)(2,1)S(1)} collective-permute-done((bf16[272,512]{1,0:T(8,128)(2,1)S(1)}, bf16[272,512]{1,0:T(8,128)(2,1)S(1)}, u32[]{:S(2)}, u32[]{:S(2)}) %collective-permute-start.4) | collective-permute-done | bytes 278560 | tf_op jit(solution)/shard_map/ppermute | solution.py:411
  55.9 1.4 %transform_columns.6 = (bf16[2,1280,256]{2,1,0:T(8,128)(2,1)S(1)}, bf16[2,16,256]{2,1,0:T(8,128)(2,1)S(1)}) custom-call(s32[1]{0:T(128)} %bitcast.odd_ref, bf16[272,512]{1,0:T(8,128)(2,1)S(1)} %collective-permute-done.mine_ref.mine_notes, bf16[272,512]{1,0:T(8,128)(2,1)S(1)} %collective-permute-done.mine_ref.mine_notes, ...), custom_call_target="tpu_custom_call" | custom-call | flops 671088640 | bytes 1310720 | tf_op jit(solution)/shard_map/transform_columns/pallas_call | solution.py:225
  57.2 1.9 %expand_rows.6 = (bf16[160,5,16,128]{3,2,1,0:T(8,128)(2,1)S(1)}, bf16[160,5,16,128]{3,2,1,0:T(8,128)(2,1)S(1)}) custom-call(bf16[2,1280,256]{2,1,0:T(8,128)(2,1)S(1)} %get-tuple-element.47.refs_0_, bf16[2,16,256]{2,1,0:T(8,128)(2,1)S(1)} %get-tuple-element.48.refs_1_), custom_call_target="tpu_custom_call" | custom-call | flops 1677721600 | bytes 6553600 | tf_op jit(solution)/shard_map/expand_rows/pallas_call | solution.py:330
  59.2 3.0 %expand_rows.7 = (bf16[160,5,16,128]{3,2,1,0:T(8,128)(2,1)S(1)}, bf16[160,5,16,128]{3,2,1,0:T(8,128)(2,1)S(1)}, bf16[160,5,16,128]{3,2,1,0:T(8,128)(2,1)S(1)}, bf16[160,5,16,128]{3,2,1,0:T(8,128)(2,1)S(1)}) custom-call(bf16[2,1280,256]{2,1,0:T(8,128)(2,1)S(1)} %get-tuple-element.45.refs_0_, bf16[2,16,256]{2,1,0:T(8,128)(2,1)S(1)} %get-tuple-element.46.refs_1_, ...), custom_call_target="tpu_custom_call" | custom-call | flops 1677721600 | bytes 6553600 | tf_op jit(solution)/shard_map/expand_rows/pallas_call | solution.py:330
  62.1 1.6 %transform_columns.4 = (bf16[2,1280,256]{2,1,0:T(8,128)(2,1)S(1)}, bf16[2,16,256]{2,1,0:T(8,128)(2,1)S(1)}) custom-call(s32[1]{0:T(128)} %bitcast.odd_ref, bf16[272,512]{1,0:T(8,128)(2,1)S(1)} %collective-permute-done.1.mine_ref.mine_notes, bf16[272,512]{1,0:T(8,128)(2,1)S(1)} %collective-permute-done.1.mine_ref.mine_notes, ...), custom_call_target="tpu_custom_call" | custom-call | flops 671088640 | bytes 1310720 | tf_op jit(solution)/shard_map/transform_columns/pallas_call | solution.py:225
  63.7 2.9 %expand_rows.5 = (bf16[160,5,16,128]{3,2,1,0:T(8,128)(2,1)S(1)}, bf16[160,5,16,128]{3,2,1,0:T(8,128)(2,1)S(1)}, bf16[160,5,16,128]{3,2,1,0:T(8,128)(2,1)S(1)}, bf16[160,5,16,128]{3,2,1,0:T(8,128)(2,1)S(1)}) custom-call(bf16[2,1280,256]{2,1,0:T(8,128)(2,1)S(1)} %get-tuple-element.38.refs_0_, bf16[2,16,256]{2,1,0:T(8,128)(2,1)S(1)} %get-tuple-element.39.refs_1_, ...), custom_call_target="tpu_custom_call" | custom-call | flops 1677721600 | bytes 6553600 | tf_op jit(solution)/shard_map/expand_rows/pallas_call | solution.py:330
  66.7 11.5 %form_image.1 = bf16[640,12800]{1,0:T(8,128)(2,1)} custom-call(bf16[160,5,16,128]{3,2,1,0:T(8,128)(2,1)S(1)} %get-tuple-element.44.refs_0_, bf16[160,5,16,128]{3,2,1,0:T(8,128)(2,1)S(1)} %get-tuple-element.51.refs_1_, bf16[160,5,16,128]{3,2,1,0:T(8,128)(2,1)S(1)} %get-tuple-element.52.refs_2_, bf16[160,5,16,128]{3,2,1,0:T(8,128)(2,1)S(1)} %get-tuple-element.53.refs_3_, ...), custom_call_target="tpu_custom_call" | custom-call | flops 8388608000 | bytes 32768000 | tf_op jit(solution)/shard_map/form_image/pallas_call | solution.py:368
  (37 shorter events, 6.2 us)
Async XLA Ops:
  0.0 14.6 %copy-start.3 = (bf16[640,1280]{1,0:T(8,128)(2,1)S(1)}, bf16[640,1280]{1,0:T(8,128)(2,1)}, u32[]{:S(2)}) copy-start(bf16[640,1280]{1,0:T(8,128)(2,1)} %constant.112.clone.wave_ref) | copy-start | bytes 4915204
  2.2 19.5 %all-to-all-start = ((bf16[32,40,128]{2,1,0:T(8,128)(2,1)}), bf16[32,40,128]{2,1,0:T(8,128)(2,1)}, u32[]{:S(2)}, u32[]{:S(2)}) async-start(bf16[32,40,128]{2,1,0:T(8,128)(2,1)} %pack_slots.1), calls=%async_computation | async-start | bytes 655360 | tf_op jit(solution)/shard_map/all_to_all | solution.py:431
  15.6 0.7 copy-start
  16.3 0.8 %copy-start.4 = (bf16[2,320,512]{2,1,0:T(8,128)(2,1)}, bf16[2,320,512]{2,1,0:T(8,128)(2,1)S(1)}, u32[]{:S(2)}) copy-start(bf16[2,320,512]{2,1,0:T(8,128)(2,1)S(1)} %get-tuple-element.58.refs_8_) | copy-start | bytes 1966084
  24.9 15.4 %collective-permute-start = (bf16[272,512]{1,0:T(8,128)(2,1)}, bf16[272,512]{1,0:T(8,128)(2,1)S(1)}, u32[]{:S(2)}, u32[]{:S(2)}) collective-permute-start(bf16[272,512]{1,0:T(8,128)(2,1)} %grid_windows.1.mine_ref.mine_notes), channel_id=1, source_target_pairs={{4,0},{5,1},{6,2},{7,3},{0,4},{1,5},{2,6},{3,7},{12,8},{13,9},{14,... | collective-permute-start | bytes 835592 | tf_op jit(solution)/shard_map/ppermute | solution.py:411
  25.0 15.4 %collective-permute-start.5 = (bf16[272,512]{1,0:T(8,128)(2,1)}, bf16[272,512]{1,0:T(8,128)(2,1)S(1)}, u32[]{:S(2)}, u32[]{:S(2)}) collective-permute-start(bf16[272,512]{1,0:T(8,128)(2,1)} %grid_windows.1.mine_ref.mine_notes), channel_id=1, source_target_pairs={{2,0},{3,1},{0,2},{1,3},{6,4},{7,5},{4,6},{5,7},{10,8},{11,9},{8,1... | collective-permute-start | bytes 835592 | tf_op jit(solution)/shard_map/ppermute | solution.py:411
  26.6 15.8 %collective-permute-start.3 = (bf16[272,512]{1,0:T(8,128)(2,1)}, bf16[272,512]{1,0:T(8,128)(2,1)S(1)}, u32[]{:S(2)}, u32[]{:S(2)}) collective-permute-start(bf16[272,512]{1,0:T(8,128)(2,1)} %grid_windows.1.mine_ref.mine_notes), channel_id=1, source_target_pairs={{1,0},{0,1},{3,2},{2,3},{5,4},{4,5},{7,6},{6,7},{9,8},{8,9},{11,10... | collective-permute-start | bytes 835592 | tf_op jit(solution)/shard_map/ppermute | solution.py:411
  40.4 7.9 %collective-permute-start.1 = (bf16[272,512]{1,0:T(8,128)(2,1)S(1)}, bf16[272,512]{1,0:T(8,128)(2,1)S(1)}, u32[]{:S(2)}, u32[]{:S(2)}) collective-permute-start(bf16[272,512]{1,0:T(8,128)(2,1)S(1)} %collective-permute-done.mine_ref.mine_notes), channel_id=1, source_target_pairs={{2,0},{3,1},{0,2},{1,3},{6,4},{7,5},{4,6},{5,7},{10,8},{11,9},{8,1... | collective-permute-start | bytes 835592 | tf_op jit(solution)/shard_map/ppermute | solution.py:411
  40.4 9.5 %collective-permute-start.6 = (bf16[272,512]{1,0:T(8,128)(2,1)S(1)}, bf16[272,512]{1,0:T(8,128)(2,1)S(1)}, u32[]{:S(2)}, u32[]{:S(2)}) collective-permute-start(bf16[272,512]{1,0:T(8,128)(2,1)S(1)} %collective-permute-done.5.mine_ref.mine_notes), channel_id=1, source_target_pairs={{1,0},{0,1},{3,2},{2,3},{5,4},{4,5},{7,6},{6,7},{9,8},{8,9},{11,10... | collective-permute-start | bytes 835592 | tf_op jit(solution)/shard_map/ppermute | solution.py:411
  41.1 14.8 %collective-permute-start.4 = (bf16[272,512]{1,0:T(8,128)(2,1)S(1)}, bf16[272,512]{1,0:T(8,128)(2,1)S(1)}, u32[]{:S(2)}, u32[]{:S(2)}) collective-permute-start(bf16[272,512]{1,0:T(8,128)(2,1)S(1)} %collective-permute-done.mine_ref.mine_notes), channel_id=1, source_target_pairs={{1,0},{0,1},{3,2},{2,3},{5,4},{4,5},{7,6},{6,7},{9,8},{8,9},{11,10... | collective-permute-start | bytes 835592 | tf_op jit(solution)/shard_map/ppermute | solution.py:411
  42.4 0.9 %copy-start.1 = (bf16[80,1280]{1,0:T(8,128)(2,1)S(1)}, bf16[80,1280]{1,0:T(8,128)(2,1)}, u32[]{:S(2)}) copy-start(bf16[80,1280]{1,0:T(8,128)(2,1)} %copy-done) | copy-start | bytes 614404
  45.6 4.3 %copy-start.2 = (bf16[80,1280]{1,0:T(8,128)(2,1)S(1)}, bf16[80,1280]{1,0:T(8,128)(2,1)}, u32[]{:S(2)}) copy-start(bf16[80,1280]{1,0:T(8,128)(2,1)} %copy-done) | copy-start | bytes 614404
  48.2 13.9 %collective-permute-start.2 = (bf16[272,512]{1,0:T(8,128)(2,1)S(1)}, bf16[272,512]{1,0:T(8,128)(2,1)S(1)}, u32[]{:S(2)}, u32[]{:S(2)}) collective-permute-start(bf16[272,512]{1,0:T(8,128)(2,1)S(1)} %collective-permute-done.1.mine_ref.mine_notes), channel_id=1, source_target_pairs={{1,0},{0,1},{3,2},{2,3},{5,4},{4,5},{7,6},{6,7},{9,8},{8,9},{11,10... | collective-permute-start | bytes 835592 | tf_op jit(solution)/shard_map/ppermute | solution.py:411
  63.7 2.9 %copy-start.5 = (bf16[2,320,512]{2,1,0:T(8,128)(2,1)S(1)}, bf16[2,320,512]{2,1,0:T(8,128)(2,1)}, u32[]{:S(2)}) copy-start(bf16[2,320,512]{2,1,0:T(8,128)(2,1)} %copy-done.4) | copy-start | bytes 1966084
